TPU v7x, 32 devices: a whole 2x2x4 slice. The times are simulated.
32 devices in a mesh: tm: 16 (over z, x, core), head: 2 (over y).
Axes of the slice: x: 2, y: 2, z: 4, core: 2. Of those that a mesh axis runs over, the one named last changes fastest.
Arguments:
- queries: bfloat16 [16, 392, 1024], P('tm', None, 'head'), may hold values from -6 to 6
- key_tokens: bfloat16 [16, 392, 1024], P('tm', None, 'head'), may hold values from -6 to 6
- value_tokens: bfloat16 [16, 392, 1024], P('tm', None, 'head'), may hold values from -6 to 6
- out_weight: bfloat16 [1024, 1024], P('head'), may hold values from -0.1875 to 0.1875
- out_grad: bfloat16 [16, 392, 1024], P('tm'), may hold values from -6 to 6
- clip_starts: int32 [16], P('tm'), may hold values from 0 to 1, as said below
Outputs:
- projected: bfloat16 [16, 392, 1024], P('tm', 'head')
- grad_queries: bfloat16 [16, 392, 1024], P('tm', None, 'head')
- grad_keys: bfloat16 [16, 392, 1024], P('tm', None, 'head')
- grad_values: bfloat16 [16, 392, 1024], P('tm', None, 'head')
Inputs may be any that keep to these rules, and one draw needn't show every extreme that they name: `clip_starts`: the last 8 clips never begin a new video.
All inputs are finite; a program needn't handle non-finite values.
Results may differ from a plain program's by a relative error of at most 0.0087.
Values may be sent and summed in bfloat16 or wider, within the bound.
A program may use at most 64 MiB of HBM per device.

v0:
```python
import functools

import jax
import jax.numpy as jnp
from jax import lax
from jax.experimental import pallas as pl
from jax.experimental.pallas import tpu as pltpu
from jax.sharding import PartitionSpec as P

HEAD_DIM = 64
POOL = 4
MEM = 8
GROUP = 4
LANES = 2 * HEAD_DIM
EXCLUDED = -1e30
F32 = jnp.float32
BF16 = jnp.bfloat16
BY_COLUMN = (((1,), (1,)), ((), ()))
BY_ROW = (((0,), (0,)), ((), ()))


def attention_kernel(
    start, q_ref, k_ref, v_ref, mem_ref, weight_ref, grad_ref,
    share_ref, dq_ref, own_ref, memory_grad_ref,
    key_ext, value_ext, bias, partial_ref,
):
    step = pl.program_id(0)
    tokens = q_ref.shape[0]
    pooled = tokens // POOL
    pitch = mem_ref.shape[2]
    base = MEM * pitch

    @pl.when(step == 0)
    def _():
        bias[...] = jnp.full(bias.shape, EXCLUDED, F32)
        running = jnp.full((1, LANES), 1 - start[0], jnp.int32).astype(F32)
        for slot in range(MEM):
            keep = mem_ref[slot, 0, pooled : pooled + 1, :].astype(F32)
            exists = mem_ref[slot, 0, pooled + 1 : pooled + 2, :].astype(F32)
            level = (1.0 - running * exists) * EXCLUDED
            bias[slot * pitch : slot * pitch + pooled, :] = jnp.broadcast_to(level, (pooled, LANES))
            running = running * keep
        bias[base : base + tokens, :] = jnp.zeros((tokens, LANES), F32)

    for slot in range(MEM):
        rows = slice(slot * pitch, (slot + 1) * pitch)
        key_ext[rows, :] = mem_ref[slot, 0].astype(F32)
        value_ext[rows, :] = mem_ref[slot, 1].astype(F32)
    key_ext[base : base + tokens, :] = k_ref[...].astype(F32)
    value_ext[base : base + tokens, :] = v_ref[...].astype(F32)

    scale = HEAD_DIM ** (-0.5)
    grad = lax.dot_general(grad_ref[...], weight_ref[...], BY_COLUMN, preferred_element_type=F32)
    query = q_ref[...].astype(F32)
    keys = key_ext[...]
    values = value_ext[...]
    key_pair = keys.astype(BF16)
    token_lane = lax.broadcasted_iota(jnp.int32, (tokens, LANES), 1)
    ext_lane = lax.broadcasted_iota(jnp.int32, keys.shape, 1)
    attended, dq, dk, dv = [], [], [], []
    for side in range(2):
        mine = (token_lane < HEAD_DIM) if side == 0 else (token_lane >= HEAD_DIM)
        mine_ext = (ext_lane < HEAD_DIM) if side == 0 else (ext_lane >= HEAD_DIM)
        spare = HEAD_DIM * (1 - side)
        query_aug = jnp.where(mine, query, jnp.where(token_lane == spare, 1.0, 0.0)).astype(BF16)
        key_aug = jnp.where(mine_ext, keys, bias[...]).astype(BF16)
        value_aug = jnp.where(mine_ext, values, 1.0).astype(BF16)
        scores = lax.dot_general(query_aug, key_aug, BY_COLUMN, preferred_element_type=F32)
        peak = jnp.max(scores, axis=1, keepdims=True)
        expo = jnp.exp((scores - peak) * scale)
        expo_low = expo.astype(BF16)
        gathered = jnp.dot(expo_low, value_aug, preferred_element_type=F32)
        inverse = 1.0 / pltpu.roll(gathered, HEAD_DIM, 1)
        attended_side = jnp.where(mine, gathered * inverse, 0.0)
        grad_side = jnp.where(mine, grad * inverse, 0.0).astype(BF16)
        delta = jnp.sum(grad_side.astype(F32) * attended_side, axis=1, keepdims=True)
        high = delta.astype(BF16).astype(F32)
        low = delta - high
        grad_aug = jnp.where(
            mine,
            grad_side.astype(F32),
            jnp.where(token_lane == spare, -high, jnp.where(token_lane == spare + 1, -low, 0.0)),
        ).astype(BF16)
        centred = lax.dot_general(grad_aug, value_aug, BY_COLUMN, preferred_element_type=F32)
        grad_scores = (expo * centred).astype(BF16)
        query_side = jnp.where(mine, query * scale, 0.0).astype(BF16)
        dq.append(jnp.dot(grad_scores, key_pair, preferred_element_type=F32))
        dk.append(lax.dot_general(grad_scores, query_side, BY_ROW, preferred_element_type=F32))
        dv.append(lax.dot_general(expo_low, grad_side, BY_ROW, preferred_element_type=F32))
        attended.append(attended_side)
    dq_ref[...] = (jnp.where(token_lane < HEAD_DIM, dq[0], dq[1]) * scale).astype(BF16)
    for which, total in enumerate((dk[0] + dk[1], dv[0] + dv[1])):
        for slot in range(MEM):
            memory_grad_ref[slot, which] = total[slot * pitch : (slot + 1) * pitch, :].astype(BF16)
        own_ref[which] = total[base : base + tokens, :]
    share = jnp.dot(
        (attended[0] + attended[1]).astype(BF16), weight_ref[...], preferred_element_type=F32
    )

    @pl.when(step == 0)
    def _():
        partial_ref[...] = share

    @pl.when(step > 0)
    def _():
        partial_ref[...] += share

    @pl.when(step == pl.num_programs(0) - 1)
    def _():
        rows = share_ref.shape[1]
        for part in range(share_ref.shape[0]):
            share_ref[part] = partial_ref[part * rows : (part + 1) * rows, :].astype(BF16)


def attention(start, queries, keys, values, memory, weight, grad, parts):
    tokens, width = queries.shape
    full = weight.shape[1]
    pitch = memory.shape[2]
    extent = MEM * pitch + tokens
    columns = pl.BlockSpec((tokens, LANES), lambda i: (0, i))
    memory_block = pl.BlockSpec((MEM, 2, pitch, LANES), lambda i: (0, 0, 0, i))
    return pl.pallas_call(
        attention_kernel,
        grid=(width // LANES,),
        in_specs=[
            pl.BlockSpec(memory_space=pltpu.SMEM),
            columns,
            columns,
            columns,
            memory_block,
            pl.BlockSpec((LANES, full), lambda i: (i, 0)),
            pl.BlockSpec((tokens, full), lambda i: (0, 0)),
        ],
        out_specs=[
            pl.BlockSpec((parts, tokens // parts, full), lambda i: (0, 0, 0)),
            columns,
            pl.BlockSpec((2, tokens, LANES), lambda i: (0, 0, i)),
            memory_block,
        ],
        out_shape=[
            jax.ShapeDtypeStruct((parts, tokens // parts, full), BF16),
            jax.ShapeDtypeStruct((tokens, width), BF16),
            jax.ShapeDtypeStruct((2, tokens, width), F32),
            jax.ShapeDtypeStruct((MEM, 2, pitch, width), BF16),
        ],
        scratch_shapes=[pltpu.VMEM((extent, LANES), F32)] * 3 + [pltpu.VMEM((tokens, full), F32)],
        compiler_params=pltpu.CompilerParams(dimension_semantics=("arbitrary",)),
        name="attention",
    )(start, queries, keys, values, memory, weight, grad)


def remote(source, target, send, receive, device):
    return pltpu.make_async_remote_copy(
        src_ref=source,
        dst_ref=target,
        send_sem=send,
        recv_sem=receive,
        device_id=device,
        device_id_type=pl.DeviceIdType.MESH,
    )


def place(count):
    me = lax.axis_index("tm")
    core = lax.rem(me, 2)
    side = lax.rem(me // 2, 2)
    sibling = {"tm": me + 1 - 2 * core}
    across = {"tm": me + 2 - 4 * side}
    later = {"tm": lax.rem(me + GROUP, count)}
    earlier = {"tm": lax.rem(me + count - GROUP, count)}
    return me, core, side, sibling, across, later, earlier, me + GROUP < count, me >= GROUP


def greet(neighbours):
    barrier = pltpu.get_barrier_semaphore()
    for device in neighbours:
        pl.semaphore_signal(
            barrier, inc=1, device_id=device, device_id_type=pl.DeviceIdType.MESH
        )
    pl.semaphore_wait(barrier, len(neighbours))


def gather_kernel(count, start, k_ref, v_ref, out_ref, buf, send, receive, stored):
    me, core, side, sibling, across, later, earlier, has_later, has_earlier = place(count)
    tokens, width = k_ref.shape
    pooled = tokens // POOL
    pitch = out_ref.shape[2]
    row = lax.broadcasted_iota(jnp.int32, (pitch, tokens), 0)
    token = lax.broadcasted_iota(jnp.int32, (pitch, tokens), 1)
    inside = (token >= row * POOL) & (token < row * POOL + POOL)
    mixing = jnp.where(inside, 1.0 / POOL, 0.0).astype(BF16)
    line = lax.broadcasted_iota(jnp.int32, (pitch, width), 0)
    keep = jnp.full((pitch, width), 1 - start[0], jnp.int32).astype(F32)
    for which, ref in enumerate((k_ref, v_ref)):
        mean = jnp.dot(mixing, ref[...], preferred_element_type=F32)
        mean = jnp.where(line == pooled, keep, jnp.where(line == pooled + 1, 1.0, mean))
        buf[0, which] = mean.astype(BF16)

    @pl.when(jnp.logical_not(has_earlier))
    def _():
        for slot in (4, 8):
            buf[slot] = jnp.zeros(buf.shape[1:], BF16)

    greet([sibling, across, later, earlier])

    def move(source, target, which, number, device):
        return remote(
            buf.at[source, which], buf.at[target, which],
            send.at[number, which], receive.at[target, which], device,
        )

    def arrive(slot, which):
        move(slot, slot, which, 0, sibling).wait_recv()

    def store(slot, which):
        pltpu.make_async_copy(
            buf.at[slot, which], out_ref.at[slot - 1, which], stored.at[slot - 1, which]
        ).start()

    for which in range(2):
        pl.when(has_later)(lambda: move(0, 4, which, 0, later).start())
        pl.when(side == 0)(lambda: move(0, 2, which, 2, across).start())
        pl.when(core == 0)(lambda: move(0, 1, which, 4, sibling).start())
    for which in range(2):
        pl.when(has_earlier)(lambda: arrive(4, which))
        pl.when(has_later)(lambda: move(4, 8, which, 1, later).start())
        pl.when(side == 0)(lambda: move(4, 6, which, 3, across).start())
        pl.when(side == 1)(lambda: move(4, 2, which, 2, across).start())
        pl.when(core == 0)(lambda: move(4, 5, which, 5, sibling).start())
        pl.when(core == 1)(lambda: move(4, 3, which, 4, sibling).start())
        store(4, which)
    for which in range(2):
        arrive(2, which)
        pl.when(core == 0)(lambda: move(2, 3, which, 6, sibling).start())
        pl.when(core == 1)(lambda: move(2, 1, which, 6, sibling).start())
        store(2, which)
    for which in range(2):
        pl.when(has_earlier)(lambda: arrive(8, which))
        pl.when(side == 1)(lambda: move(8, 6, which, 3, across).start())
        pl.when(core == 1)(lambda: move(8, 7, which, 5, sibling).start())
        store(8, which)
    for which in range(2):
        arrive(6, which)
        pl.when(core == 0)(lambda: move(6, 7, which, 7, sibling).start())
        pl.when(core == 1)(lambda: move(6, 5, which, 7, sibling).start())
        store(6, which)
    for slot in (1, 3, 5, 7):
        for which in range(2):
            arrive(slot, which)
            store(slot, which)
    for which in range(2):
        for number in (0, 1):
            pl.when(has_later)(lambda: move(0, 4, which, number, later).wait_send())
        for number in range(2, 8):
            move(0, 2, which, number, across).wait_send()
        for slot in range(1, MEM + 1):
            pltpu.make_async_copy(
                buf.at[slot, which], out_ref.at[slot - 1, which], stored.at[slot - 1, which]
            ).wait()


def gather(start, keys, values, count):
    tokens, width = keys.shape
    pitch = -(-(tokens // POOL + 2) // 8) * 8
    whole = pl.BlockSpec(memory_space=pltpu.VMEM)
    return pl.pallas_call(
        functools.partial(gather_kernel, count),
        in_specs=[pl.BlockSpec(memory_space=pltpu.SMEM), whole, whole],
        out_specs=pl.BlockSpec(memory_space=pl.ANY),
        out_shape=jax.ShapeDtypeStruct((MEM, 2, pitch, width), BF16),
        scratch_shapes=[
            pltpu.VMEM((MEM + 1, 2, pitch, width), BF16),
            pltpu.SemaphoreType.DMA((8, 2)),
            pltpu.SemaphoreType.DMA((MEM + 1, 2)),
            pltpu.SemaphoreType.DMA((MEM, 2)),
        ],
        compiler_params=pltpu.CompilerParams(collective_id=1, has_side_effects=True),
        name="gather",
    )(start, keys, values)


def giving_kernel(
    count, parts, grads, share_ref, projected_ref, returned_ref,
    landed, sums, shares, send, receive, share_send, share_receive,
):
    me, core, side, sibling, across, later, earlier, has_later, has_earlier = place(count)
    head = lax.axis_index("head")

    @pl.when(jnp.logical_not(has_later))
    def _():
        for number in (6, 7):
            landed[number] = jnp.zeros(landed.shape[1:], BF16)

    peers = [{"head": lax.rem(head + k, parts)} for k in range(1, parts)]
    greet([sibling, across, later, earlier] + peers)

    def move(source, number, which, device):
        return remote(
            source, landed.at[number, which],
            send.at[number, which], receive.at[number, which], device,
        )

    def slot(index, which):
        return grads.at[index - 1, which]

    for which in range(2):
        for number, bottom, step in ((3, 5, 2), (1, 7, -2), (2, 1, 2), (0, 3, -2)):
            move(slot(bottom + step * core, which), number, which, sibling).start()
    exchanges = []
    for k, peer in enumerate(peers):
        copy = remote(
            share_ref.at[lax.rem(head + k + 1, parts)], shares.at[k],
            share_send.at[k], share_receive.at[k], peer,
        )
        copy.start()
        exchanges.append(copy)

    def arrive(number, which):
        move(slot(1, which), number, which, sibling).wait_recv()
        return landed[number, which].astype(F32)

    is_core = core.astype(F32)
    is_side = side.astype(F32)
    for which in range(2):
        sums[1, which] = (grads[5, which].astype(F32) + arrive(3, which)).astype(BF16)
        move(sums.at[1, which], 5, which, across).start()
    for which in range(2):
        from_core = arrive(1, which)
        sums[0, which] = (grads[1, which].astype(F32) + arrive(2, which)).astype(BF16)
        move(sums.at[0, which], 4, which, across).start()
    for which in range(2):
        total = grads[7, which].astype(F32) + is_core * landed[1, which].astype(F32)
        total = total + is_side * arrive(5, which)
        sums[3, which] = total.astype(BF16)
        pl.when(has_earlier)(lambda: move(sums.at[3, which], 7, which, earlier).start())
    for which in range(2):
        total = grads[3, which].astype(F32) + (1 - is_core) * landed[1, which].astype(F32)
        total = total + is_core * arrive(0, which)
        total = total + (1 - is_side) * landed[5, which].astype(F32)
        total = total + is_side * arrive(4, which)
        pl.when(has_later)(
            lambda: move(slot(1, which), 7, which, sibling).wait_recv()
        )
        total = total + landed[7, which].astype(F32)
        sums[2, which] = total.astype(BF16)
        pl.when(has_earlier)(lambda: move(sums.at[2, which], 6, which, earlier).start())

    for copy in exchanges:
        copy.wait()
    projected = share_ref[head].astype(F32)
    for k in range(parts - 1):
        projected = projected + shares[k].astype(F32)
    projected_ref[...] = projected.astype(BF16)

    for which in range(2):
        pl.when(has_later)(
            lambda: move(slot(1, which), 6, which, sibling).wait_recv()
        )
        total = (1 - is_core) * landed[0, which].astype(F32) + landed[6, which].astype(F32)
        total = total + (1 - is_side) * landed[4, which].astype(F32)
        returned_ref[which] = total.astype(BF16)
    for which in range(2):
        for number in range(6):
            move(slot(1, which), number, which, sibling).wait_send()
        for number in (6, 7):
            pl.when(has_earlier)(
                lambda: move(slot(1, which), number, which, sibling).wait_send()
            )


def give_back(grads, share, count):
    parts, rows, full = share.shape
    pitch, width = grads.shape[2:]
    whole = pl.BlockSpec(memory_space=pltpu.VMEM)
    return pl.pallas_call(
        functools.partial(giving_kernel, count, parts),
        in_specs=[whole] * 2,
        out_specs=[whole] * 2,
        out_shape=[
            jax.ShapeDtypeStruct((rows, full), BF16),
            jax.ShapeDtypeStruct((2, pitch, width), BF16),
        ],
        scratch_shapes=[
            pltpu.VMEM((8, 2, pitch, width), BF16),
            pltpu.VMEM((4, 2, pitch, width), BF16),
            pltpu.VMEM((parts - 1, rows, full), BF16),
            pltpu.SemaphoreType.DMA((8, 2)),
            pltpu.SemaphoreType.DMA((8, 2)),
            pltpu.SemaphoreType.DMA((parts - 1,)),
            pltpu.SemaphoreType.DMA((parts - 1,)),
        ],
        compiler_params=pltpu.CompilerParams(collective_id=2, has_side_effects=True),
        name="give_back",
    )(grads, share)


def finish_kernel(own_ref, returned_ref, share_ref, projected_ref, dk_ref, dv_ref):
    tokens = own_ref.shape[1]
    pitch = returned_ref.shape[1]
    token = lax.broadcasted_iota(jnp.int32, (tokens, pitch), 0)
    row = lax.broadcasted_iota(jnp.int32, (tokens, pitch), 1)
    inside = (token >= row * POOL) & (token < row * POOL + POOL)
    spread = jnp.where(inside, 1.0 / POOL, 0.0).astype(BF16)
    for which, ref in enumerate((dk_ref, dv_ref)):
        shared = jnp.dot(spread, returned_ref[which], preferred_element_type=F32)
        ref[...] = (own_ref[which] + shared).astype(BF16)
    projected_ref[...] = share_ref[...]


def finish(own, returned, share):
    _, tokens, width = own.shape
    pitch = returned.shape[1]
    rows, full = share.shape
    steps = width // LANES
    columns = pl.BlockSpec((tokens, LANES), lambda i: (0, i))
    shares = pl.BlockSpec((rows, full // steps), lambda i: (0, i))
    return pl.pallas_call(
        finish_kernel,
        grid=(steps,),
        in_specs=[
            pl.BlockSpec((2, tokens, LANES), lambda i: (0, 0, i)),
            pl.BlockSpec((2, pitch, LANES), lambda i: (0, 0, i)),
            shares,
        ],
        out_specs=[shares, columns, columns],
        out_shape=[
            jax.ShapeDtypeStruct((rows, full), BF16),
            jax.ShapeDtypeStruct((tokens, width), BF16),
            jax.ShapeDtypeStruct((tokens, width), BF16),
        ],
        compiler_params=pltpu.CompilerParams(dimension_semantics=("arbitrary",)),
        name="finish",
    )(own, returned, share)


def local(queries, key_tokens, value_tokens, out_weight, out_grad, clip_starts):
    count = lax.axis_size("tm")
    memory = gather(clip_starts, key_tokens[0], value_tokens[0], count)
    share, dq, own, memory_grads = attention(
        clip_starts, queries[0], key_tokens[0], value_tokens[0], memory, out_weight, out_grad[0],
        lax.axis_size("head"),
    )
    share, returned = give_back(memory_grads, share, count)
    projected, dk, dv = finish(own, returned, share)
    return (projected[None], dq[None], dk[None], dv[None])


def solution(mesh):
    return jax.shard_map(
        local,
        mesh=mesh,
        in_specs=(
            P("tm", None, "head"),
            P("tm", None, "head"),
            P("tm", None, "head"),
            P("head", None),
            P("tm", None, None),
            P("tm"),
        ),
        out_specs=(
            P("tm", "head", None),
            P("tm", None, "head"),
            P("tm", None, "head"),
            P("tm", None, "head"),
        ),
        check_vma=False,
    )
```

profile of v0, /device:TPU:0, one launch (start us, length us, event | category | flops | bytes accessed | tf_op | source)
XLA Modules:
  0.0 77.4 jit_solution(3200119777707729927)
XLA Ops:
  1.3 19.9 %gather.1.mem_ref = bf16[8,2,104,512]{3,2,1,0:T(8,128)(2,1)} custom-call(s32[1]{0:T(128)S(6)} %copy.10.start, bf16[392,512]{1,0:T(8,128)(2,1)} %bitcast.8, bf16[392,512]{1,0:T(8,128)(2,1)} %bitcast.10), custom_call_target="tpu_custom_call" | custom-call | tf_op jit(solution)/shard_map/gather/pallas_call | solution.py:266
  21.2 28.0 %attention.1 = (bf16[2,196,1024]{2,1,0:T(8,128)(2,1)}, bf16[392,512]{1,0:T(8,128)(2,1)}, f32[2,392,512]{2,1,0:T(8,128)}, bf16[8,2,104,512]{3,2,1,0:T(8,128)(2,1)}) custom-call(s32[1]{0:T(128)S(6)} %copy.10.start, bf16[392,512]{1,0:T(8,128)(2,1)} %bitcast.13, bf16[392,512]{1,0:T(8,128)(2,1)} %bitcast.9, bf16[392,512]{1,0:T(8,128)(2,1)} %bitcast.11, ...), custom_call_target="tpu_custom_call" | custom-call | tf_op jit(solution)/shard_map/attention/pallas_call | solution.py:122
  49.2 24.1 %give_back.1 = (bf16[196,1024]{1,0:T(8,128)(2,1)}, bf16[2,104,512]{2,1,0:T(8,128)(2,1)}) custom-call(bf16[8,2,104,512]{3,2,1,0:T(8,128)(2,1)} %get-tuple-element.14.grads, bf16[2,196,1024]{2,1,0:T(8,128)(2,1)} %get-tuple-element.15.share_ref), custom_call_target="tpu_custom_call" | custom-call | tf_op jit(solution)/shard_map/give_back/pallas_call | solution.py:375
  73.3 4.0 %finish.1 = (bf16[196,1024]{1,0:T(8,128)(2,1)}, bf16[392,512]{1,0:T(8,128)(2,1)}, bf16[392,512]{1,0:T(8,128)(2,1)}) custom-call(f32[2,392,512]{2,1,0:T(8,128)} %get-tuple-element.13.own_ref, bf16[2,104,512]{2,1,0:T(8,128)(2,1)} %get-tuple-element.16.returned_ref, bf16[196,1024]{1,0:T(8,128)(2,1)} %get-tuple-element.17.share_ref), custom_call_target="tpu_custom_call" | custom-call | tf_op jit(solution)/shard_map/finish/pallas_call | solution.py:417
where the time goes:
time: 77.6 us; the launch traced here: 77.4 us
  Pallas kernels  76.1 us (98%)
  between operations  1.29 us (2%)
    pallas_call x1, Pallas kernels, attention(): pl.pallas_call(attention_kernel, grid=(width // LANES,), in_specs=[pl.Blo...  28 us
    pallas_call x1, Pallas kernels, give_back(): pl.pallas_call(functools.partial(giving_kernel, count, parts), in_specs=[...  24.1 us
    pallas_call x1, Pallas kernels, gather(): pl.pallas_call(functools.partial(gather_kernel, count), in_specs=[pl.Bloc...  19.9 us
    pallas_call x1, Pallas kernels, finish(): pl.pallas_call(finish_kernel, grid=(steps,), in_specs=[pl.BlockSpec((2, t...  4.02 us

commit v1 on v0

--- a/solution.py
+++ b/solution.py
@@ -29,72 +29,80 @@
     pooled = tokens // POOL
     pitch = mem_ref.shape[2]
     base = MEM * pitch
+    extent = key_ext.shape[0]
 
     @pl.when(step == 0)
     def _():
-        bias[...] = jnp.full(bias.shape, EXCLUDED, F32)
+        bias[...] = jnp.full(bias.shape, EXCLUDED, BF16)
         running = jnp.full((1, LANES), 1 - start[0], jnp.int32).astype(F32)
         for slot in range(MEM):
             keep = mem_ref[slot, 0, pooled : pooled + 1, :].astype(F32)
             exists = mem_ref[slot, 0, pooled + 1 : pooled + 2, :].astype(F32)
-            level = (1.0 - running * exists) * EXCLUDED
+            level = ((1.0 - running * exists) * EXCLUDED).astype(BF16)
             bias[slot * pitch : slot * pitch + pooled, :] = jnp.broadcast_to(level, (pooled, LANES))
             running = running * keep
-        bias[base : base + tokens, :] = jnp.zeros((tokens, LANES), F32)
+        bias[base : base + tokens, :] = jnp.zeros((tokens, LANES), BF16)
+        key_ext[base + tokens :, :] = jnp.zeros((extent - base - tokens, LANES), BF16)
+        value_ext[base + tokens :, :] = jnp.zeros((extent - base - tokens, LANES), BF16)
 
     for slot in range(MEM):
         rows = slice(slot * pitch, (slot + 1) * pitch)
-        key_ext[rows, :] = mem_ref[slot, 0].astype(F32)
-        value_ext[rows, :] = mem_ref[slot, 1].astype(F32)
-    key_ext[base : base + tokens, :] = k_ref[...].astype(F32)
-    value_ext[base : base + tokens, :] = v_ref[...].astype(F32)
+        key_ext[rows, :] = mem_ref[slot, 0]
+        value_ext[rows, :] = mem_ref[slot, 1]
+    key_ext[base : base + tokens, :] = k_ref[...]
+    value_ext[base : base + tokens, :] = v_ref[...]
 
     scale = HEAD_DIM ** (-0.5)
-    grad = lax.dot_general(grad_ref[...], weight_ref[...], BY_COLUMN, preferred_element_type=F32)
-    query = q_ref[...].astype(F32)
+    grad_t = lax.dot_general(weight_ref[...], grad_ref[...], BY_COLUMN, preferred_element_type=F32)
+    query = q_ref[...]
     keys = key_ext[...]
     values = value_ext[...]
-    key_pair = keys.astype(BF16)
+    key_t = keys.T
+    value_t = values.T
+    query_t = (query * scale).T
     token_lane = lax.broadcasted_iota(jnp.int32, (tokens, LANES), 1)
     ext_lane = lax.broadcasted_iota(jnp.int32, keys.shape, 1)
+    ones = jnp.ones((16, extent), BF16)
+    line = lax.broadcasted_iota(jnp.int32, (HEAD_DIM, tokens), 0)
     attended, dq, dk, dv = [], [], [], []
     for side in range(2):
         mine = (token_lane < HEAD_DIM) if side == 0 else (token_lane >= HEAD_DIM)
         mine_ext = (ext_lane < HEAD_DIM) if side == 0 else (ext_lane >= HEAD_DIM)
+        head = slice(side * HEAD_DIM, (side + 1) * HEAD_DIM)
         spare = HEAD_DIM * (1 - side)
-        query_aug = jnp.where(mine, query, jnp.where(token_lane == spare, 1.0, 0.0)).astype(BF16)
-        key_aug = jnp.where(mine_ext, keys, bias[...]).astype(BF16)
-        value_aug = jnp.where(mine_ext, values, 1.0).astype(BF16)
+        query_aug = jnp.where(mine, query, jnp.where(token_lane == spare, 1.0, 0.0).astype(BF16))
+        key_aug = jnp.where(mine_ext, keys, bias[...])
+        value_aug = jnp.where(mine_ext, values, jnp.ones_like(values))
         scores = lax.dot_general(query_aug, key_aug, BY_COLUMN, preferred_element_type=F32)
         peak = jnp.max(scores, axis=1, keepdims=True)
         expo = jnp.exp((scores - peak) * scale)
         expo_low = expo.astype(BF16)
-        gathered = jnp.dot(expo_low, value_aug, preferred_element_type=F32)
-        inverse = 1.0 / pltpu.roll(gathered, HEAD_DIM, 1)
-        attended_side = jnp.where(mine, gathered * inverse, 0.0)
-        grad_side = jnp.where(mine, grad * inverse, 0.0).astype(BF16)
-        delta = jnp.sum(grad_side.astype(F32) * attended_side, axis=1, keepdims=True)
+        moving = jnp.concatenate([value_t[head, :], ones], axis=0)
+        gathered = lax.dot_general(moving, expo_low, BY_COLUMN, preferred_element_type=F32)
+        inverse = 1.0 / gathered[HEAD_DIM : HEAD_DIM + 1, :]
+        attended_side = gathered[:HEAD_DIM, :] * inverse
+        grad_side = (grad_t[head, :] * inverse).astype(BF16)
+        delta = jnp.sum(grad_side.astype(F32) * attended_side, axis=0, keepdims=True)
         high = delta.astype(BF16).astype(F32)
         low = delta - high
-        grad_aug = jnp.where(
-            mine,
-            grad_side.astype(F32),
-            jnp.where(token_lane == spare, -high, jnp.where(token_lane == spare + 1, -low, 0.0)),
-        ).astype(BF16)
+        extra = jnp.where(line == 0, -high, jnp.where(line == 1, -low, 0.0)).astype(BF16)
+        pair = [grad_side, extra] if side == 0 else [extra, grad_side]
+        grad_aug = jnp.concatenate(pair, axis=0).T
         centred = lax.dot_general(grad_aug, value_aug, BY_COLUMN, preferred_element_type=F32)
         grad_scores = (expo * centred).astype(BF16)
-        query_side = jnp.where(mine, query * scale, 0.0).astype(BF16)
-        dq.append(jnp.dot(grad_scores, key_pair, preferred_element_type=F32))
-        dk.append(lax.dot_general(grad_scores, query_side, BY_ROW, preferred_element_type=F32))
-        dv.append(lax.dot_general(expo_low, grad_side, BY_ROW, preferred_element_type=F32))
+        dv.append(jnp.dot(grad_side, expo_low, preferred_element_type=F32))
+        dk.append(jnp.dot(query_t[head, :], grad_scores, preferred_element_type=F32))
+        dq.append(lax.dot_general(key_t[head, :], grad_scores, BY_COLUMN, preferred_element_type=F32))
         attended.append(attended_side)
-    dq_ref[...] = (jnp.where(token_lane < HEAD_DIM, dq[0], dq[1]) * scale).astype(BF16)
-    for which, total in enumerate((dk[0] + dk[1], dv[0] + dv[1])):
+    dq_ref[...] = (jnp.concatenate(dq, axis=0) * scale).astype(BF16).T
+    for which, parts in enumerate((dk, dv)):
+        total = jnp.concatenate(parts, axis=0)
+        memory = total[:, : base].astype(BF16).T
         for slot in range(MEM):
-            memory_grad_ref[slot, which] = total[slot * pitch : (slot + 1) * pitch, :].astype(BF16)
-        own_ref[which] = total[base : base + tokens, :]
+            memory_grad_ref[slot, which] = memory[slot * pitch : (slot + 1) * pitch, :]
+        own_ref[which] = total[:, base : ].T[:tokens, :]
     share = jnp.dot(
-        (attended[0] + attended[1]).astype(BF16), weight_ref[...], preferred_element_type=F32
+        jnp.concatenate(attended, axis=0).astype(BF16).T, weight_ref[...], preferred_element_type=F32
     )
 
     @pl.when(step == 0)
@@ -116,7 +124,7 @@
     tokens, width = queries.shape
     full = weight.shape[1]
     pitch = memory.shape[2]
-    extent = MEM * pitch + tokens
+    extent = -(-(MEM * pitch + tokens) // LANES) * LANES
     columns = pl.BlockSpec((tokens, LANES), lambda i: (0, i))
     memory_block = pl.BlockSpec((MEM, 2, pitch, LANES), lambda i: (0, 0, 0, i))
     return pl.pallas_call(
@@ -143,7 +151,7 @@
             jax.ShapeDtypeStruct((2, tokens, width), F32),
             jax.ShapeDtypeStruct((MEM, 2, pitch, width), BF16),
         ],
-        scratch_shapes=[pltpu.VMEM((extent, LANES), F32)] * 3 + [pltpu.VMEM((tokens, full), F32)],
+        scratch_shapes=[pltpu.VMEM((extent, LANES), BF16)] * 3 + [pltpu.VMEM((tokens, full), F32)],
         compiler_params=pltpu.CompilerParams(dimension_semantics=("arbitrary",)),
         name="attention",
     )(start, queries, keys, values, memory, weight, grad)

time: 77.6 us -> 71.6 us (0.923)
  Pallas kernels: 76.1 us -> 70 us
    pallas_call x1, Pallas kernels: 28 us -> 22 us  [attention(): pl.pallas_call(attention_kernel, grid=(width // LANES,), in_specs=[pl.Blo...]
where the time goes in v1:
time: 71.6 us; the launch traced here: 71.3 us
  Pallas kernels  70 us (98%)
  between operations  1.29 us (2%)
    pallas_call x1, Pallas kernels, give_back(): pl.pallas_call(functools.partial(giving_kernel, count, parts), in_specs=[...  24.1 us
    pallas_call x1, Pallas kernels, attention(): pl.pallas_call(attention_kernel, grid=(width // LANES,), in_specs=[pl.Blo...  22 us
    pallas_call x1, Pallas kernels, gather(): pl.pallas_call(functools.partial(gather_kernel, count), in_specs=[pl.Bloc...  19.9 us
    pallas_call x1, Pallas kernels, finish(): pl.pallas_call(finish_kernel, grid=(steps,), in_specs=[pl.BlockSpec((2, t...  4.02 us

profile of v1, /device:TPU:0, one launch (start us, length us, event | category | flops | bytes accessed | tf_op | source)
XLA Modules:
  0.0 71.3 jit_solution(3157539013620136826)
XLA Ops:
  1.3 19.9 %gather.1.mem_ref = bf16[8,2,104,512]{3,2,1,0:T(8,128)(2,1)} custom-call(s32[1]{0:T(128)S(6)} %copy.10.start, bf16[392,512]{1,0:T(8,128)(2,1)} %bitcast.8, bf16[392,512]{1,0:T(8,128)(2,1)} %bitcast.10), custom_call_target="tpu_custom_call" | custom-call | tf_op jit(solution)/shard_map/gather/pallas_call | solution.py:274
  21.2 22.0 %attention.1 = (bf16[2,196,1024]{2,1,0:T(8,128)(2,1)}, bf16[392,512]{1,0:T(8,128)(2,1)}, f32[2,392,512]{2,1,0:T(8,128)}, bf16[8,2,104,512]{3,2,1,0:T(8,128)(2,1)}) custom-call(s32[1]{0:T(128)S(6)} %copy.10.start, bf16[392,512]{1,0:T(8,128)(2,1)} %bitcast.13, bf16[392,512]{1,0:T(8,128)(2,1)} %bitcast.9, bf16[392,512]{1,0:T(8,128)(2,1)} %bitcast.11, ...), custom_call_target="tpu_custom_call" | custom-call | tf_op jit(solution)/shard_map/attention/pallas_call | solution.py:130
  43.2 24.1 %give_back.1 = (bf16[196,1024]{1,0:T(8,128)(2,1)}, bf16[2,104,512]{2,1,0:T(8,128)(2,1)}) custom-call(bf16[8,2,104,512]{3,2,1,0:T(8,128)(2,1)} %get-tuple-element.14.grads, bf16[2,196,1024]{2,1,0:T(8,128)(2,1)} %get-tuple-element.15.share_ref), custom_call_target="tpu_custom_call" | custom-call | tf_op jit(solution)/shard_map/give_back/pallas_call | solution.py:383
  67.3 4.0 %finish.1 = (bf16[196,1024]{1,0:T(8,128)(2,1)}, bf16[392,512]{1,0:T(8,128)(2,1)}, bf16[392,512]{1,0:T(8,128)(2,1)}) custom-call(f32[2,392,512]{2,1,0:T(8,128)} %get-tuple-element.13.own_ref, bf16[2,104,512]{2,1,0:T(8,128)(2,1)} %get-tuple-element.16.returned_ref, bf16[196,1024]{1,0:T(8,128)(2,1)} %get-tuple-element.17.share_ref), custom_call_target="tpu_custom_call" | custom-call | tf_op jit(solution)/shard_map/finish/pallas_call | solution.py:425

commit v2 on v0

v2 whole, which is shorter than its diff:
```python
import functools

import jax
import jax.numpy as jnp
from jax import lax
from jax.experimental import pallas as pl
from jax.experimental.pallas import tpu as pltpu
from jax.sharding import PartitionSpec as P

HEAD_DIM = 64
POOL = 4
MEM = 8
GROUP = 4
LANES = 2 * HEAD_DIM
EXCLUDED = -1e30
F32 = jnp.float32
BF16 = jnp.bfloat16
BY_COLUMN = (((1,), (1,)), ((), ()))


def remote(source, target, send, receive, device):
    return pltpu.make_async_remote_copy(
        src_ref=source,
        dst_ref=target,
        send_sem=send,
        recv_sem=receive,
        device_id=device,
        device_id_type=pl.DeviceIdType.MESH,
    )


def place(count):
    me = lax.axis_index("tm")
    core = lax.rem(me, 2)
    side = lax.rem(me // 2, 2)
    sibling = {"tm": me + 1 - 2 * core}
    across = {"tm": me + 2 - 4 * side}
    later = {"tm": lax.rem(me + GROUP, count)}
    earlier = {"tm": lax.rem(me + count - GROUP, count)}
    return me, core, side, sibling, across, later, earlier, me + GROUP < count, me >= GROUP


def kernel(
    count, parts, start, q_in, k_in, v_in, weight_in, grad_in,
    projected, dq_out, dk_out, dv_out,
    q, k, v, grad, weights, mem, key_ext, value_ext, bias, grad_t,
    own, grads, landed, sums, att, att_in, dq_buf, out_buf, projected_buf,
    loads, gsend, greceive, bsend, breceive, wsend, wreceive, fsend, freceive,
    asend, areceive, stores,
):
    me, core, side, sibling, across, later, earlier, has_later, has_earlier = place(count)
    head = lax.axis_index("head")
    tokens, width = q.shape
    full = grad.shape[1]
    chunks = width // LANES
    pooled = tokens // POOL
    pitch = mem.shape[3]
    base = MEM * pitch
    extent = key_ext.shape[0]
    rows = tokens // parts
    half = width // 2
    scale = HEAD_DIM ** (-0.5)

    def load(number, source, target):
        return pltpu.make_async_copy(source, target, loads.at[number])

    inputs = [
        load(0, k_in, k), load(1, v_in, v), load(2, weight_in, weights.at[head]),
        load(3, grad_in, grad), load(4, q_in, q),
    ]
    for copy in inputs:
        copy.start()

    peers = [{"head": lax.rem(head + n, parts)} for n in range(1, parts)]
    barrier = pltpu.get_barrier_semaphore()
    neighbours = [sibling, across, later, earlier] + peers
    for device in neighbours:
        pl.semaphore_signal(barrier, inc=1, device_id=device, device_id_type=pl.DeviceIdType.MESH)

    row = lax.broadcasted_iota(jnp.int32, (pitch, tokens), 0)
    token = lax.broadcasted_iota(jnp.int32, (pitch, tokens), 1)
    inside = (token >= row * POOL) & (token < row * POOL + POOL)
    mixing = jnp.where(inside, 1.0 / POOL, 0.0).astype(BF16)
    line = lax.broadcasted_iota(jnp.int32, (pitch, width), 0)
    keep = jnp.full((pitch, width), 1 - start[0], jnp.int32).astype(F32)
    for which, ref in enumerate((k, v)):
        inputs[which].wait()
        mean = jnp.dot(mixing, ref[...], preferred_element_type=F32)
        mean = jnp.where(line == pooled, keep, jnp.where(line == pooled + 1, 1.0, mean)).astype(BF16)
        for c in range(chunks):
            mem[c, 0, which] = mean[:, c * LANES : (c + 1) * LANES]

    @pl.when(jnp.logical_not(has_earlier))
    def _():
        for slot in (4, 8):
            for c in range(chunks):
                mem[c, slot] = jnp.zeros(mem.shape[2:], BF16)

    @pl.when(jnp.logical_not(has_later))
    def _():
        for number in (6, 7):
            for c in range(chunks):
                landed[c, number] = jnp.zeros(landed.shape[2:], BF16)

    pl.semaphore_wait(barrier, len(neighbours))

    def move(c, source, target, number, device):
        return remote(
            mem.at[c, source], mem.at[c, target],
            gsend.at[c, number], greceive.at[c, target], device,
        )

    def arrive(c, slot):
        move(c, slot, slot, 0, sibling).wait_recv()

    def send_own(c):
        pl.when(has_later)(lambda: move(c, 0, 4, 0, later).start())
        pl.when(side == 0)(lambda: move(c, 0, 2, 2, across).start())
        pl.when(core == 0)(lambda: move(c, 0, 1, 4, sibling).start())

    def relay_four(c):
        pl.when(has_earlier)(lambda: arrive(c, 4))
        pl.when(has_later)(lambda: move(c, 4, 8, 1, later).start())
        move(c, 4, 6 - 4 * side, 3 - side, across).start()
        move(c, 4, 5 - 2 * core, 5 - core, sibling).start()

    def relay_two_and_eight(c):
        arrive(c, 2)
        move(c, 2, 3 - 2 * core, 6, sibling).start()
        pl.when(has_earlier)(lambda: arrive(c, 8))
        pl.when(side == 1)(lambda: move(c, 8, 6, 3, across).start())
        pl.when(core == 1)(lambda: move(c, 8, 7, 5, sibling).start())

    def relay_six(c):
        arrive(c, 6)
        move(c, 6, 7 - 2 * core, 7, sibling).start()

    def gathered_all(c):
        for slot in (1, 3, 5, 7):
            arrive(c, slot)

    def gather_sent(c):
        for number in (0, 1):
            pl.when(has_later)(lambda: move(c, 0, 4, number, later).wait_send())
        for number in range(2, 8):
            move(c, 0, 2, number, across).wait_send()

    def give(c, source, number, device):
        return remote(
            source, landed.at[c, number], bsend.at[c, number], breceive.at[c, number], device
        )

    def got(c, number):
        give(c, grads.at[c, 0], number, sibling).wait_recv()

    is_core = core.astype(F32)
    is_side = side.astype(F32)

    def term(c, number):
        return landed[c, number].astype(F32)

    def give_siblings(c):
        for number, bottom, step in ((3, 5, 2), (1, 7, -2), (2, 1, 2), (0, 3, -2)):
            give(c, grads.at[c, bottom + step * core - 1], number, sibling).start()

    def give_across(c):
        got(c, 3)
        sums[c, 1] = (grads[c, 5].astype(F32) + term(c, 3)).astype(BF16)
        give(c, sums.at[c, 1], 5, across).start()
        got(c, 2)
        sums[c, 0] = (grads[c, 1].astype(F32) + term(c, 2)).astype(BF16)
        give(c, sums.at[c, 0], 4, across).start()

    def give_eight(c):
        got(c, 1)
        got(c, 5)
        total = grads[c, 7].astype(F32) + is_core * term(c, 1) + is_side * term(c, 5)
        sums[c, 3] = total.astype(BF16)
        pl.when(has_earlier)(lambda: give(c, sums.at[c, 3], 7, earlier).start())

    def give_four(c):
        got(c, 0)
        got(c, 4)
        total = grads[c, 3].astype(F32) + (1 - is_core) * term(c, 1) + is_core * term(c, 0)
        total = total + (1 - is_side) * term(c, 5) + is_side * term(c, 4)
        pl.when(has_later)(lambda: got(c, 7))
        total = total + term(c, 7)
        sums[c, 2] = total.astype(BF16)
        pl.when(has_earlier)(lambda: give(c, sums.at[c, 2], 6, earlier).start())

    def columns(c):
        return pl.ds(pl.multiple_of(c * LANES, LANES), LANES)

    def store(c, number, source, target):
        return pltpu.make_async_copy(source, target.at[:, columns(c)], stores.at[c, number])

    spread_token = lax.broadcasted_iota(jnp.int32, (tokens, pitch), 0)
    spread_row = lax.broadcasted_iota(jnp.int32, (tokens, pitch), 1)
    spread_inside = (spread_token >= spread_row * POOL) & (spread_token < spread_row * POOL + POOL)

    def finish(c):
        pl.when(has_later)(lambda: got(c, 6))
        total = (1 - is_core) * term(c, 0) + term(c, 6) + (1 - is_side) * term(c, 4)
        total = total.astype(BF16)
        spread = jnp.where(spread_inside, 1.0 / POOL, 0.0).astype(BF16)
        for which, target in enumerate((dk_out, dv_out)):
            shared = jnp.dot(spread, total[which], preferred_element_type=F32)
            out_buf[c, which] = (own[c, which] + shared).astype(BF16)
            store(c, which, out_buf.at[c, which], target).start()

    def given(c):
        for number in range(6):
            give(c, grads.at[c, 0], number, sibling).wait_send()
        for number in (6, 7):
            pl.when(has_earlier)(lambda: give(c, grads.at[c, 0], number, sibling).wait_send())

    def weight_out(n):
        mine = weights.at[head, pl.ds(core * half, half)]
        return remote(mine, mine, wsend.at[n - 1], wreceive.at[n - 1], peers[n - 1])

    def weight_on(n):
        theirs = weights.at[lax.rem(head + parts - n, parts), pl.ds(core * half, half)]
        return remote(theirs, theirs, fsend.at[n - 1], freceive.at[n - 1], sibling)

    def attended_out(c, n):
        return remote(
            att.at[lax.rem(head + n, parts), :, columns(c)], att_in.at[head, :, columns(c)],
            asend.at[c, n - 1], areceive.at[c, n - 1], peers[n - 1],
        )

    send_own(0)
    if chunks > 1:
        send_own(1)
    inputs[2].wait()
    for n in range(1, parts):
        weight_out(n).start()
    relay_four(0)
    inputs[3].wait()
    grad_t[...] = lax.dot_general(
        weights[head], grad[...], BY_COLUMN, preferred_element_type=F32
    ).reshape(grad_t.shape)
    relay_two_and_eight(0)
    bias[...] = jnp.full(bias.shape, EXCLUDED, BF16)
    bias[base : base + tokens, :] = jnp.zeros((tokens, LANES), BF16)
    key_ext[base + tokens :, :] = jnp.zeros((extent - base - tokens, LANES), BF16)
    value_ext[base + tokens :, :] = jnp.zeros((extent - base - tokens, LANES), BF16)
    inputs[4].wait()
    relay_six(0)
    gathered_all(0)
    running = jnp.full((1, LANES), 1 - start[0], jnp.int32).astype(F32)
    for slot in range(MEM):
        keep_slot = mem[0, slot + 1, 0, pooled : pooled + 1, :].astype(F32)
        exists = mem[0, slot + 1, 0, pooled + 1 : pooled + 2, :].astype(F32)
        level = ((1.0 - running * exists) * EXCLUDED).astype(BF16)
        bias[slot * pitch : slot * pitch + pooled, :] = jnp.broadcast_to(level, (pooled, LANES))
        running = running * keep_slot

    def step(i, carry):
        @pl.when(i > 0)
        def _():
            gathered_all(i)
            give_across(i - 1)

        @pl.when(i + 1 < chunks)
        def _():
            relay_four(i + 1)

        for slot in range(MEM):
            lines = slice(slot * pitch, (slot + 1) * pitch)
            key_ext[lines, :] = mem[i, slot + 1, 0]
            value_ext[lines, :] = mem[i, slot + 1, 1]
        key_ext[base : base + tokens, :] = k[:, columns(i)]
        value_ext[base : base + tokens, :] = v[:, columns(i)]

        token_lane = lax.broadcasted_iota(jnp.int32, (tokens, LANES), 1)
        ext_lane = lax.broadcasted_iota(jnp.int32, (extent, LANES), 1)
        ones = jnp.ones((16, extent), BF16)
        extra_line = lax.broadcasted_iota(jnp.int32, (HEAD_DIM, tokens), 0)
        query = q[:, columns(i)]
        query_t = (query * scale).T
        keys = key_ext[...]
        values = value_ext[...]
        key_t = keys.T
        value_t = values.T
        attended, dq, dk, dv = [], [], [], []
        for which_head in range(2):
            mine = (token_lane < HEAD_DIM) if which_head == 0 else (token_lane >= HEAD_DIM)
            mine_ext = (ext_lane < HEAD_DIM) if which_head == 0 else (ext_lane >= HEAD_DIM)
            lines = slice(which_head * HEAD_DIM, (which_head + 1) * HEAD_DIM)
            spare = HEAD_DIM * (1 - which_head)
            query_aug = jnp.where(mine, query, jnp.where(token_lane == spare, 1.0, 0.0).astype(BF16))
            key_aug = jnp.where(mine_ext, keys, bias[...])
            value_aug = jnp.where(mine_ext, values, jnp.ones_like(values))
            scores = lax.dot_general(query_aug, key_aug, BY_COLUMN, preferred_element_type=F32)
            peak = jnp.max(scores, axis=1, keepdims=True)
            expo = jnp.exp((scores - peak) * scale)
            expo_low = expo.astype(BF16)
            moving = jnp.concatenate([value_t[lines, :], ones], axis=0)
            gathered = lax.dot_general(moving, expo_low, BY_COLUMN, preferred_element_type=F32)
            inverse = 1.0 / gathered[HEAD_DIM : HEAD_DIM + 1, :]
            attended_side = gathered[:HEAD_DIM, :] * inverse
            grad_side = (grad_t[i, lines, :] * inverse).astype(BF16)
            delta = jnp.sum(grad_side.astype(F32) * attended_side, axis=0, keepdims=True)
            high = delta.astype(BF16).astype(F32)
            low = delta - high
            extra = jnp.where(extra_line == 0, -high, jnp.where(extra_line == 1, -low, 0.0)).astype(BF16)
            pair = [grad_side, extra] if which_head == 0 else [extra, grad_side]
            grad_aug = jnp.concatenate(pair, axis=0).T
            centred = lax.dot_general(grad_aug, value_aug, BY_COLUMN, preferred_element_type=F32)
            grad_scores = (expo * centred).astype(BF16)
            dv.append(jnp.dot(grad_side, expo_low, preferred_element_type=F32))
            dk.append(jnp.dot(query_t[lines, :], grad_scores, preferred_element_type=F32))
            dq.append(lax.dot_general(key_t[lines, :], grad_scores, BY_COLUMN, preferred_element_type=F32))
            attended.append(attended_side)
            if which_head == 0:
                @pl.when(i > 0)
                def _():
                    give_eight(i - 1)

                @pl.when(i + 1 < chunks)
                def _():
                    relay_two_and_eight(i + 1)

        totals = [jnp.concatenate(pair, axis=0) for pair in (dk, dv)]
        for which, total in enumerate(totals):
            memory = total[:, :base].astype(BF16).T
            for slot in range(MEM):
                grads[i, slot, which] = memory[slot * pitch : (slot + 1) * pitch, :]
        attended = jnp.concatenate(attended, axis=0).astype(BF16).T
        for part in range(parts):
            att[part, :, columns(i)] = attended[part * rows : (part + 1) * rows, :]
        give_siblings(i)
        for n in range(1, parts):
            attended_out(i, n).start()

        @pl.when(i > 0)
        def _():
            give_four(i - 1)

        @pl.when(i + 1 < chunks)
        def _():
            relay_six(i + 1)

        @pl.when(i + 2 < chunks)
        def _():
            send_own(i + 2)

        for which, total in enumerate(totals):
            own[i, which] = total[:, base:].T[:tokens, :]
        dq_buf[i] = (jnp.concatenate(dq, axis=0) * scale).astype(BF16).T
        store(i, 2, dq_buf.at[i], dq_out).start()

        @pl.when(i > 0)
        def _():
            finish(i - 1)

        @pl.when(i == min(1, chunks - 1))
        def _():
            for n in range(1, parts):
                weight_out(n).wait_recv()
                weight_on(n).start()

        gather_sent(i)
        return carry

    lax.fori_loop(0, chunks, step, 0)

    last = chunks - 1
    give_across(last)
    total = jnp.dot(att[head], weights[head], preferred_element_type=F32)
    for n in range(1, parts):
        weight_on(n).wait_recv()
        for c in range(chunks):
            attended_out(c, n).wait_recv()
    give_eight(last)
    for n in range(1, parts):
        other = lax.rem(head + n, parts)
        total = total + jnp.dot(att_in[other], weights[other], preferred_element_type=F32)
    projected_buf[...] = total.astype(BF16)
    final = pltpu.make_async_copy(projected_buf, projected, loads.at[5])
    final.start()
    give_four(last)
    for c in range(chunks - 1):
        given(c)
        for number in range(3):
            store(c, number, dq_buf.at[c], dq_out).wait()
    for n in range(1, parts):
        weight_out(n).wait_send()
        weight_on(n).wait_send()
        for c in range(chunks):
            attended_out(c, n).wait_send()
    finish(last)
    given(last)
    for number in range(3):
        store(last, number, dq_buf.at[last], dq_out).wait()
    final.wait()


def whole(queries, key_tokens, value_tokens, out_weight, out_grad, start, count, parts):
    tokens, width = queries.shape
    full = out_weight.shape[1]
    chunks = width // LANES
    rows = tokens // parts
    pitch = -(-(tokens // POOL + 2) // 8) * 8
    extent = -(-(MEM * pitch + tokens) // LANES) * LANES
    anywhere = pl.BlockSpec(memory_space=pl.ANY)
    dma = pltpu.SemaphoreType.DMA
    return pl.pallas_call(
        functools.partial(kernel, count, parts),
        in_specs=[pl.BlockSpec(memory_space=pltpu.SMEM)] + [anywhere] * 5,
        out_specs=[anywhere] * 4,
        out_shape=[
            jax.ShapeDtypeStruct((rows, full), BF16),
            jax.ShapeDtypeStruct((tokens, width), BF16),
            jax.ShapeDtypeStruct((tokens, width), BF16),
            jax.ShapeDtypeStruct((tokens, width), BF16),
        ],
        scratch_shapes=[
            pltpu.VMEM((tokens, width), BF16),
            pltpu.VMEM((tokens, width), BF16),
            pltpu.VMEM((tokens, width), BF16),
            pltpu.VMEM((tokens, full), BF16),
            pltpu.VMEM((parts, width, full), BF16),
            pltpu.VMEM((chunks, MEM + 1, 2, pitch, LANES), BF16),
            pltpu.VMEM((extent, LANES), BF16),
            pltpu.VMEM((extent, LANES), BF16),
            pltpu.VMEM((extent, LANES), BF16),
            pltpu.VMEM((chunks, LANES, tokens), F32),
            pltpu.VMEM((chunks, 2, tokens, LANES), F32),
            pltpu.VMEM((chunks, MEM, 2, pitch, LANES), BF16),
            pltpu.VMEM((chunks, 8, 2, pitch, LANES), BF16),
            pltpu.VMEM((chunks, 4, 2, pitch, LANES), BF16),
            pltpu.VMEM((parts, rows, width), BF16),
            pltpu.VMEM((parts, rows, width), BF16),
            pltpu.VMEM((chunks, tokens, LANES), BF16),
            pltpu.VMEM((chunks, 2, tokens, LANES), BF16),
            pltpu.VMEM((rows, full), BF16),
            dma((6,)),
            dma((chunks, 8)),
            dma((chunks, MEM + 1)),
            dma((chunks, 8)),
            dma((chunks, 8)),
            dma((parts - 1,)),
            dma((parts - 1,)),
            dma((parts - 1,)),
            dma((parts - 1,)),
            dma((chunks, parts - 1)),
            dma((chunks, parts - 1)),
            dma((chunks, 3)),
        ],
        compiler_params=pltpu.CompilerParams(collective_id=1, has_side_effects=True),
        name="attention",
    )(start, queries, key_tokens, value_tokens, out_weight, out_grad)


def local(queries, key_tokens, value_tokens, out_weight, out_grad, clip_starts):
    projected, dq, dk, dv = whole(
        queries[0], key_tokens[0], value_tokens[0], out_weight, out_grad[0], clip_starts,
        lax.axis_size("tm"), lax.axis_size("head"),
    )
    return (projected[None], dq[None], dk[None], dv[None])


def solution(mesh):
    return jax.shard_map(
        local,
        mesh=mesh,
        in_specs=(
            P("tm", None, "head"),
            P("tm", None, "head"),
            P("tm", None, "head"),
            P("head", None),
            P("tm", None, None),
            P("tm"),
        ),
        out_specs=(
            P("tm", "head", None),
            P("tm", None, "head"),
            P("tm", None, "head"),
            P("tm", None, "head"),
        ),
        check_vma=False,
    )
```

time: 77.6 us -> 66.7 us (0.86)
  Pallas kernels: 76.1 us -> 60.3 us
  local copies, waits for them, and re-layouts: 0 us -> 4.87 us
    pallas_call x4 -> x1, Pallas kernels: 76.1 us -> 60.3 us  [whole(): pl.pallas_call(functools.partial(kernel, count, parts), in_specs=[pl.Bloc...]
    unnamed x0 -> x10, local copies, waits for them, and re-layouts: none -> 4.87 us
where the time goes in v2:
time: 66.7 us; the launch traced here: 66.5 us
  Pallas kernels  60.3 us (90%)
  local copies, waits for them, and re-layouts  4.87 us (7%)
  between operations  1.3 us (2%)
    pallas_call x1, Pallas kernels, whole(): pl.pallas_call(functools.partial(kernel, count, parts), in_specs=[pl.Bloc...  60.3 us
    unnamed x10, local copies, waits for them, and re-layouts  4.87 us

profile of v2, /device:TPU:0, one launch (start us, length us, event | category | flops | bytes accessed | tf_op | source)
XLA Modules:
  0.0 66.5 jit_solution(15664060947825428032)
XLA Ops:
  1.3 60.3 %attention.1 = (bf16[196,1024]{1,0:T(8,128)(2,1)}, bf16[392,512]{1,0:T(8,128)(2,1)}, bf16[392,512]{1,0:T(8,128)(2,1)}, bf16[392,512]{1,0:T(8,128)(2,1)}) custom-call(s32[1]{0:T(128)S(6)} %copy.14.start, bf16[392,512]{1,0:T(8,128)(2,1)} %bitcast.10, bf16[392,512]{1,0:T(8,128)(2,1)} %bitcast.11, bf16[392,512]{1,0:T(8,128)(2,1)} %bitcast.12, ...), custom_call_target="tpu_custom_call" | custom-call | tf_op jit(solution)/shard_map/attention/pallas_call | solution.py:408
  61.6 0.0 copy-start.2
  61.6 1.8 %copy.15 = bf16[1,196,1024]{2,1,0:T(8,128)(2,1)} copy(bf16[1,196,1024]{2,1,0:T(8,128)(2,1)} %bitcast.9) | data formatting | bytes 802816
  63.4 0.0 copy-done.2
  63.4 0.0 copy-start.1
  63.5 0.7 %copy.16 = bf16[1,392,512]{2,1,0:T(8,128)(2,1)} copy(bf16[1,392,512]{2,1,0:T(8,128)(2,1)S(1)} %bitcast.15) | data formatting | bytes 802816
  64.2 0.4 copy-done.1
  64.6 0.0 copy-start
  64.6 0.7 %copy.17 = bf16[1,392,512]{2,1,0:T(8,128)(2,1)} copy(bf16[1,392,512]{2,1,0:T(8,128)(2,1)S(1)} %bitcast.14) | data formatting | bytes 802816
  65.3 0.4 copy-done
  65.7 0.7 %copy.18 = bf16[1,392,512]{2,1,0:T(8,128)(2,1)} copy(bf16[1,392,512]{2,1,0:T(8,128)(2,1)S(1)} %bitcast.13) | data formatting | bytes 802816
Async XLA Ops:
  61.6 1.8 %copy-start.2 = (bf16[392,512]{1,0:T(8,128)(2,1)S(1)}, bf16[392,512]{1,0:T(8,128)(2,1)}, u32[]{:S(2)}) copy-start(bf16[392,512]{1,0:T(8,128)(2,1)} %get-tuple-element.9) | copy-start | bytes 1204228
  63.4 1.1 %copy-start.1 = (bf16[392,512]{1,0:T(8,128)(2,1)S(1)}, bf16[392,512]{1,0:T(8,128)(2,1)}, u32[]{:S(2)}) copy-start(bf16[392,512]{1,0:T(8,128)(2,1)} %get-tuple-element.10) | copy-start | bytes 1204228
  64.6 1.1 %copy-start = (bf16[392,512]{1,0:T(8,128)(2,1)S(1)}, bf16[392,512]{1,0:T(8,128)(2,1)}, u32[]{:S(2)}) copy-start(bf16[392,512]{1,0:T(8,128)(2,1)} %get-tuple-element.11) | copy-start | bytes 1204228

commit v3 on v2

--- a/solution.py
+++ b/solution.py
@@ -43,8 +43,9 @@
 def kernel(
     count, parts, start, q_in, k_in, v_in, weight_in, grad_in,
     projected, dq_out, dk_out, dv_out,
-    q, k, v, grad, weights, mem, key_ext, value_ext, bias, grad_t,
-    own, grads, landed, sums, att, att_in, dq_buf, out_buf, projected_buf,
+    q, k, v, grad, weights, mem, keys, values, bias, grad_t,
+    query_t, key_own_t, own_probs, own_out, own_peak, own_grad, dq_part,
+    own, grads, landed, sums, totals, att, att_in, dq_buf, out_buf, projected_buf,
     loads, gsend, greceive, bsend, breceive, wsend, wreceive, fsend, freceive,
     asend, areceive, stores,
 ):
@@ -56,7 +57,6 @@
     pooled = tokens // POOL
     pitch = mem.shape[3]
     base = MEM * pitch
-    extent = key_ext.shape[0]
     rows = tokens // parts
     half = width // 2
     scale = HEAD_DIM ** (-0.5)
@@ -228,24 +228,101 @@
             asend.at[c, n - 1], areceive.at[c, n - 1], peers[n - 1],
         )
 
-    send_own(0)
-    if chunks > 1:
-        send_own(1)
+    def mine(lane, h):
+        return (lane < HEAD_DIM) if h == 0 else (lane >= HEAD_DIM)
+
+    def lines(h):
+        return slice(h * HEAD_DIM, (h + 1) * HEAD_DIM)
+
+    def stacked(h, first, second):
+        return jnp.concatenate([first, second] if h == 0 else [second, first], axis=0)
+
+    spare_line = lax.broadcasted_iota(jnp.int32, (HEAD_DIM, tokens), 0)
+
+    def query_side(c, h, level):
+        spare = jnp.where(spare_line == 0, level, 0.0).astype(BF16)
+        return stacked(h, query_t[c, lines(h), :], spare)
+
+    def weighted(h, value_t, low):
+        moving = jnp.concatenate([value_t, jnp.ones((16, low.shape[0]), BF16)], axis=0)
+        return jnp.dot(moving, low, preferred_element_type=F32)
+
+    def grad_sides(h, inverse, delta, c):
+        side = (grad_t[c, lines(h), :] * inverse).astype(BF16)
+        high = delta.astype(BF16).astype(F32)
+        low = delta - high
+        spare = jnp.where(spare_line == 0, -high, jnp.where(spare_line == 1, -low, 0.0)).astype(BF16)
+        return stacked(h, side, spare)
+
+    def marked(block, h, fill):
+        lane = lax.broadcasted_iota(jnp.int32, block.shape, 1)
+        return jnp.where(mine(lane, h), block, fill)
+
+    def by_column(first, second):
+        return lax.dot_general(first, second, BY_COLUMN, preferred_element_type=F32)
+
+    def own_forward(c, carry):
+        query_t[c] = (q[:, columns(c)] * scale).T
+        key = k[:, columns(c)]
+        key_own_t[c] = key.T
+        value_t = v[:, columns(c)].T
+        scores = [jnp.dot(key, query_side(c, h, 0.0), preferred_element_type=F32) for h in range(2)]
+        for h in range(2):
+            top = jnp.max(scores[h], axis=0, keepdims=True)
+            own_peak[c, h : h + 1, :] = top
+            low = jnp.exp(scores[h] - top).astype(BF16)
+            own_probs[c, h] = low
+            own_out[c, h] = weighted(h, value_t[lines(h), :], low)
+        return carry
+
+    def own_backward(c, carry):
+        value = v[:, columns(c)]
+        centred = []
+        for h in range(2):
+            centred.append(jnp.dot(marked(value, h, jnp.ones_like(value)), own_grad[c, h], preferred_element_type=F32))
+        dk, dv, dq = [], [], []
+        for h in range(2):
+            low = own_probs[c, h]
+            grad_scores = (low.astype(F32) * centred[h]).astype(BF16)
+            dv.append(by_column(own_grad[c, h, lines(h), :], low))
+            dk.append(by_column(query_t[c, lines(h), :], grad_scores))
+            dq.append(jnp.dot(key_own_t[c, lines(h), :], grad_scores, preferred_element_type=F32))
+        for which, parts_ in enumerate((dk, dv)):
+            own[c, which] = jnp.concatenate(parts_, axis=0).T
+        total = jnp.concatenate(dq, axis=0) + dq_part[c]
+        dq_buf[c] = (total * scale).astype(BF16).T
+        store(c, 2, dq_buf.at[c], dq_out).start()
+        return carry
+
+    for c in range(min(2, chunks)):
+        send_own(c)
     inputs[2].wait()
     for n in range(1, parts):
         weight_out(n).start()
-    relay_four(0)
     inputs[3].wait()
     grad_t[...] = lax.dot_general(
         weights[head], grad[...], BY_COLUMN, preferred_element_type=F32
     ).reshape(grad_t.shape)
+    inputs[4].wait()
+    middle = chunks // 2
+    lax.fori_loop(0, middle, own_forward, 0)
+    relay_four(0)
+    if chunks > 2:
+        send_own(2)
+    lax.fori_loop(middle, chunks, own_forward, 0)
+    if chunks > 1:
+        relay_four(1)
+    for c in range(3, chunks):
+        send_own(c)
+    bias[...] = jnp.full(bias.shape, EXCLUDED, BF16)
     relay_two_and_eight(0)
-    bias[...] = jnp.full(bias.shape, EXCLUDED, BF16)
-    bias[base : base + tokens, :] = jnp.zeros((tokens, LANES), BF16)
-    key_ext[base + tokens :, :] = jnp.zeros((extent - base - tokens, LANES), BF16)
-    value_ext[base + tokens :, :] = jnp.zeros((extent - base - tokens, LANES), BF16)
-    inputs[4].wait()
+    if chunks > 2:
+        relay_four(2)
+    if chunks > 1:
+        relay_two_and_eight(1)
     relay_six(0)
+    for c in range(3, chunks):
+        relay_four(c)
     gathered_all(0)
     running = jnp.full((1, LANES), 1 - start[0], jnp.int32).astype(F32)
     for slot in range(MEM):
@@ -259,83 +336,81 @@
         @pl.when(i > 0)
         def _():
             gathered_all(i)
-            give_across(i - 1)
-
-        @pl.when(i + 1 < chunks)
-        def _():
-            relay_four(i + 1)
 
         for slot in range(MEM):
-            lines = slice(slot * pitch, (slot + 1) * pitch)
-            key_ext[lines, :] = mem[i, slot + 1, 0]
-            value_ext[lines, :] = mem[i, slot + 1, 1]
-        key_ext[base : base + tokens, :] = k[:, columns(i)]
-        value_ext[base : base + tokens, :] = v[:, columns(i)]
-
-        token_lane = lax.broadcasted_iota(jnp.int32, (tokens, LANES), 1)
-        ext_lane = lax.broadcasted_iota(jnp.int32, (extent, LANES), 1)
-        ones = jnp.ones((16, extent), BF16)
-        extra_line = lax.broadcasted_iota(jnp.int32, (HEAD_DIM, tokens), 0)
-        query = q[:, columns(i)]
-        query_t = (query * scale).T
-        keys = key_ext[...]
-        values = value_ext[...]
-        key_t = keys.T
-        value_t = values.T
-        attended, dq, dk, dv = [], [], [], []
-        for which_head in range(2):
-            mine = (token_lane < HEAD_DIM) if which_head == 0 else (token_lane >= HEAD_DIM)
-            mine_ext = (ext_lane < HEAD_DIM) if which_head == 0 else (ext_lane >= HEAD_DIM)
-            lines = slice(which_head * HEAD_DIM, (which_head + 1) * HEAD_DIM)
-            spare = HEAD_DIM * (1 - which_head)
-            query_aug = jnp.where(mine, query, jnp.where(token_lane == spare, 1.0, 0.0).astype(BF16))
-            key_aug = jnp.where(mine_ext, keys, bias[...])
-            value_aug = jnp.where(mine_ext, values, jnp.ones_like(values))
-            scores = lax.dot_general(query_aug, key_aug, BY_COLUMN, preferred_element_type=F32)
-            peak = jnp.max(scores, axis=1, keepdims=True)
-            expo = jnp.exp((scores - peak) * scale)
-            expo_low = expo.astype(BF16)
-            moving = jnp.concatenate([value_t[lines, :], ones], axis=0)
-            gathered = lax.dot_general(moving, expo_low, BY_COLUMN, preferred_element_type=F32)
-            inverse = 1.0 / gathered[HEAD_DIM : HEAD_DIM + 1, :]
-            attended_side = gathered[:HEAD_DIM, :] * inverse
-            grad_side = (grad_t[i, lines, :] * inverse).astype(BF16)
-            delta = jnp.sum(grad_side.astype(F32) * attended_side, axis=0, keepdims=True)
-            high = delta.astype(BF16).astype(F32)
-            low = delta - high
-            extra = jnp.where(extra_line == 0, -high, jnp.where(extra_line == 1, -low, 0.0)).astype(BF16)
-            pair = [grad_side, extra] if which_head == 0 else [extra, grad_side]
-            grad_aug = jnp.concatenate(pair, axis=0).T
-            centred = lax.dot_general(grad_aug, value_aug, BY_COLUMN, preferred_element_type=F32)
-            grad_scores = (expo * centred).astype(BF16)
-            dv.append(jnp.dot(grad_side, expo_low, preferred_element_type=F32))
-            dk.append(jnp.dot(query_t[lines, :], grad_scores, preferred_element_type=F32))
-            dq.append(lax.dot_general(key_t[lines, :], grad_scores, BY_COLUMN, preferred_element_type=F32))
-            attended.append(attended_side)
-            if which_head == 0:
-                @pl.when(i > 0)
-                def _():
-                    give_eight(i - 1)
-
-                @pl.when(i + 1 < chunks)
-                def _():
-                    relay_two_and_eight(i + 1)
-
-        totals = [jnp.concatenate(pair, axis=0) for pair in (dk, dv)]
-        for which, total in enumerate(totals):
-            memory = total[:, :base].astype(BF16).T
-            for slot in range(MEM):
-                grads[i, slot, which] = memory[slot * pitch : (slot + 1) * pitch, :]
-        attended = jnp.concatenate(attended, axis=0).astype(BF16).T
-        for part in range(parts):
-            att[part, :, columns(i)] = attended[part * rows : (part + 1) * rows, :]
-        give_siblings(i)
-        for n in range(1, parts):
-            attended_out(i, n).start()
-
-        @pl.when(i > 0)
-        def _():
-            give_four(i - 1)
+            rows_ = slice(slot * pitch, (slot + 1) * pitch)
+            keys[rows_, :] = mem[i, slot + 1, 0]
+            values[rows_, :] = mem[i, slot + 1, 1]
+        key_t = keys[...].T
+        value_t = values[...].T
+        block = 2 * pitch
+        blocks = [slice(n * block, (n + 1) * block) for n in range(MEM // 2)]
+        count_ = len(blocks)
+        scores, low, out, dq, gside, centred, gs = {}, {}, {}, {}, {}, {}, {}
+        qside = [query_side(i, h, 1.0) for h in range(2)]
+        top = [None, None]
+        attended = [None, None]
+
+        def score(h, n):
+            key = marked(keys[blocks[n], :], h, bias[blocks[n], :])
+            scores[h, n] = jnp.dot(key, qside[h], preferred_element_type=F32)
+
+        def peak(h):
+            best = own_peak[i, h : h + 1, :]
+            for n in range(count_):
+                best = jnp.maximum(best, jnp.max(scores[h, n], axis=0, keepdims=True))
+            top[h] = best
+
+        def expo(h, n):
+            low[h, n] = jnp.exp(scores[h, n] - top[h]).astype(BF16)
+
+        def mix(h, n):
+            part = weighted(h, value_t[lines(h), blocks[n]], low[h, n])
+            out[h] = part if n == 0 else out[h] + part
+
+        def turn(h):
+            shift = jnp.exp(own_peak[i, h : h + 1, :] - top[h])
+            total = out[h] + own_out[i, h] * shift
+            inverse = 1.0 / total[HEAD_DIM : HEAD_DIM + 1, :]
+            attended[h] = total[:HEAD_DIM, :] * inverse
+            side = (grad_t[i, lines(h), :] * inverse).astype(BF16)
+            delta = jnp.sum(side.astype(F32) * attended[h], axis=0, keepdims=True)
+            gside[h] = grad_sides(h, inverse, delta, i)
+            own_grad[i, h] = grad_sides(h, inverse * shift, delta * shift, i)
+
+        def centre(h, n):
+            block_ = values[blocks[n], :]
+            value = marked(block_, h, jnp.ones_like(block_))
+            centred[h, n] = jnp.dot(value, gside[h], preferred_element_type=F32)
+
+        def grad_score(h, n):
+            gs[h, n] = (low[h, n].astype(F32) * centred[h, n]).astype(BF16)
+
+        def value_grad(h, n):
+            totals[1, lines(h), blocks[n]] = by_column(gside[h][lines(h), :], low[h, n])
+
+        def key_grad(h, n):
+            totals[0, lines(h), blocks[n]] = by_column(query_t[i, lines(h), :], gs[h, n])
+            part = jnp.dot(key_t[lines(h), blocks[n]], gs[h, n], preferred_element_type=F32)
+            dq[h] = part if n == 0 else dq[h] + part
+
+        def give_block(n):
+            for which in range(2):
+                both = totals[which, :, blocks[n]].astype(BF16).T
+                for slot in range(2):
+                    grads[i, 2 * n + slot, which] = both[slot * pitch : (slot + 1) * pitch, :]
+
+        for n in range(count_):
+            score(0, n)
+        peak(0)
+        for n in range(count_):
+            score(1, n)
+            expo(0, n)
+            if n > 0:
+                mix(0, n - 1)
+        mix(0, count_ - 1)
+        peak(1)
+        turn(0)
 
         @pl.when(i + 1 < chunks)
         def _():
@@ -343,16 +418,51 @@
 
         @pl.when(i + 2 < chunks)
         def _():
-            send_own(i + 2)
-
-        for which, total in enumerate(totals):
-            own[i, which] = total[:, base:].T[:tokens, :]
-        dq_buf[i] = (jnp.concatenate(dq, axis=0) * scale).astype(BF16).T
-        store(i, 2, dq_buf.at[i], dq_out).start()
+            relay_two_and_eight(i + 2)
 
         @pl.when(i > 0)
         def _():
-            finish(i - 1)
+            give_across(i - 1)
+
+        @pl.when(i > 1)
+        def _():
+            give_eight(i - 2)
+
+        @pl.when(i > 2)
+        def _():
+            give_four(i - 3)
+
+        centre(0, 0)
+        for n in range(count_):
+            if n + 1 < count_:
+                centre(0, n + 1)
+            expo(1, n)
+            value_grad(0, n)
+            grad_score(0, n)
+            mix(1, n)
+            if n > 0:
+                key_grad(0, n - 1)
+        turn(1)
+        key_grad(0, count_ - 1)
+        both = jnp.concatenate(attended, axis=0).astype(BF16).T
+        for part in range(parts):
+            att[part, :, columns(i)] = both[part * rows : (part + 1) * rows, :]
+        for n in range(1, parts):
+            attended_out(i, n).start()
+
+        centre(1, 0)
+        for n in range(count_):
+            if n + 1 < count_:
+                centre(1, n + 1)
+            value_grad(1, n)
+            grad_score(1, n)
+            if n > 0:
+                key_grad(1, n - 1)
+        key_grad(1, count_ - 1)
+        for n in range(count_):
+            give_block(n)
+        give_siblings(i)
+        dq_part[i] = jnp.concatenate([dq[0], dq[1]], axis=0)
 
         @pl.when(i == min(1, chunks - 1))
         def _():
@@ -366,19 +476,31 @@
     lax.fori_loop(0, chunks, step, 0)
 
     last = chunks - 1
+    if chunks > 1:
+        give_eight(last - 1)
+    if chunks > 2:
+        give_four(last - 2)
+    lax.fori_loop(0, middle, own_backward, 0)
     give_across(last)
+    if chunks > 1:
+        give_four(last - 1)
+    lax.fori_loop(middle, chunks, own_backward, 0)
+    for c in range(chunks - 2):
+        finish(c)
+    give_eight(last)
     total = jnp.dot(att[head], weights[head], preferred_element_type=F32)
     for n in range(1, parts):
         weight_on(n).wait_recv()
         for c in range(chunks):
             attended_out(c, n).wait_recv()
-    give_eight(last)
     for n in range(1, parts):
         other = lax.rem(head + n, parts)
         total = total + jnp.dot(att_in[other], weights[other], preferred_element_type=F32)
     projected_buf[...] = total.astype(BF16)
     final = pltpu.make_async_copy(projected_buf, projected, loads.at[5])
     final.start()
+    if chunks > 1:
+        finish(last - 1)
     give_four(last)
     for c in range(chunks - 1):
         given(c)
@@ -402,19 +524,18 @@
     chunks = width // LANES
     rows = tokens // parts
     pitch = -(-(tokens // POOL + 2) // 8) * 8
-    extent = -(-(MEM * pitch + tokens) // LANES) * LANES
     anywhere = pl.BlockSpec(memory_space=pl.ANY)
     dma = pltpu.SemaphoreType.DMA
     return pl.pallas_call(
         functools.partial(kernel, count, parts),
         in_specs=[pl.BlockSpec(memory_space=pltpu.SMEM)] + [anywhere] * 5,
-        out_specs=[anywhere] * 4,
-        out_shape=[
+        out_specs=[pl.BlockSpec(memory_space=pltpu.VMEM)] * 4,
+        out_shape=[pltpu.VMEM(s_.shape, s_.dtype) for s_ in [
             jax.ShapeDtypeStruct((rows, full), BF16),
             jax.ShapeDtypeStruct((tokens, width), BF16),
             jax.ShapeDtypeStruct((tokens, width), BF16),
             jax.ShapeDtypeStruct((tokens, width), BF16),
-        ],
+        ]],
         scratch_shapes=[
             pltpu.VMEM((tokens, width), BF16),
             pltpu.VMEM((tokens, width), BF16),
@@ -422,14 +543,22 @@
             pltpu.VMEM((tokens, full), BF16),
             pltpu.VMEM((parts, width, full), BF16),
             pltpu.VMEM((chunks, MEM + 1, 2, pitch, LANES), BF16),
-            pltpu.VMEM((extent, LANES), BF16),
-            pltpu.VMEM((extent, LANES), BF16),
-            pltpu.VMEM((extent, LANES), BF16),
+            pltpu.VMEM((MEM * pitch, LANES), BF16),
+            pltpu.VMEM((MEM * pitch, LANES), BF16),
+            pltpu.VMEM((MEM * pitch, LANES), BF16),
+            pltpu.VMEM((chunks, LANES, tokens), F32),
+            pltpu.VMEM((chunks, LANES, tokens), BF16),
+            pltpu.VMEM((chunks, LANES, tokens), BF16),
+            pltpu.VMEM((chunks, 2, tokens, tokens), BF16),
+            pltpu.VMEM((chunks, 2, HEAD_DIM + 16, tokens), F32),
+            pltpu.VMEM((chunks, 2, tokens), F32),
+            pltpu.VMEM((chunks, 2, LANES, tokens), BF16),
             pltpu.VMEM((chunks, LANES, tokens), F32),
             pltpu.VMEM((chunks, 2, tokens, LANES), F32),
             pltpu.VMEM((chunks, MEM, 2, pitch, LANES), BF16),
             pltpu.VMEM((chunks, 8, 2, pitch, LANES), BF16),
             pltpu.VMEM((chunks, 4, 2, pitch, LANES), BF16),
+            pltpu.VMEM((2, LANES, MEM * pitch), F32),
             pltpu.VMEM((parts, rows, width), BF16),
             pltpu.VMEM((parts, rows, width), BF16),
             pltpu.VMEM((chunks, tokens, LANES), BF16),

time: 66.7 us -> 51 us (0.76)
  Pallas kernels: 60.3 us -> 46.5 us
  local copies, waits for them, and re-layouts: 4.87 us -> 3 us
    pallas_call x1, Pallas kernels: 60.3 us -> 46.5 us  [whole(): pl.pallas_call(functools.partial(kernel, count, parts), in_specs=[pl.Bloc...]
    unnamed x10 -> x4, local copies, waits for them, and re-layouts: 4.87 us -> 3 us
where the time goes in v3:
time: 51 us; the launch traced here: 50.8 us
  Pallas kernels  46.5 us (91%)
  local copies, waits for them, and re-layouts  3 us (6%)
  between operations  1.29 us (3%)
    pallas_call x1, Pallas kernels, whole(): pl.pallas_call(functools.partial(kernel, count, parts), in_specs=[pl.Bloc...  46.5 us
    unnamed x4, local copies, waits for them, and re-layouts  3 us

profile of v3, /device:TPU:0, one launch (start us, length us, event | category | flops | bytes accessed | tf_op | source)
XLA Modules:
  0.0 50.8 jit_solution(9159501009096842190)
XLA Ops:
  1.3 46.5 %attention.1 = (bf16[196,1024]{1,0:T(8,128)(2,1)S(1)}, bf16[392,512]{1,0:T(8,128)(2,1)S(1)}, bf16[392,512]{1,0:T(8,128)(2,1)S(1)}, bf16[392,512]{1,0:T(8,128)(2,1)S(1)}) custom-call(s32[1]{0:T(128)S(6)} %copy.18.start, bf16[392,512]{1,0:T(8,128)(2,1)} %bitcast.13, bf16[392,512]{1,0:T(8,128)(2,1)} %bitcast.14, bf16[392,512]{1,0:T(8,128)(2,1)} %bitcast.15, ...), custom_call_target="tpu_custom_call" | custom-call | tf_op jit(solution)/shard_map/attention/pallas_call | solution.py:529
  47.8 0.8 %copy.14 = bf16[1,196,1024]{2,1,0:T(8,128)(2,1)} copy(bf16[1,196,1024]{2,1,0:T(8,128)(2,1)S(1)} %bitcast.8) | data formatting | bytes 802816
  48.6 0.7 %copy.15 = bf16[1,392,512]{2,1,0:T(8,128)(2,1)} copy(bf16[1,392,512]{2,1,0:T(8,128)(2,1)S(1)} %bitcast.11) | data formatting | bytes 802816
  49.3 0.7 %copy.16 = bf16[1,392,512]{2,1,0:T(8,128)(2,1)} copy(bf16[1,392,512]{2,1,0:T(8,128)(2,1)S(1)} %bitcast.10) | data formatting | bytes 802816
  50.1 0.7 %copy.17 = bf16[1,392,512]{2,1,0:T(8,128)(2,1)} copy(bf16[1,392,512]{2,1,0:T(8,128)(2,1)S(1)} %bitcast.9) | data formatting | bytes 802816

commit v4 on v3

--- a/solution.py
+++ b/solution.py
@@ -16,6 +16,7 @@
 F32 = jnp.float32
 BF16 = jnp.bfloat16
 BY_COLUMN = (((1,), (1,)), ((), ()))
+BY_ROW = (((0,), (0,)), ((), ()))
 
 
 def remote(source, target, send, receive, device):
@@ -35,9 +36,11 @@
     side = lax.rem(me // 2, 2)
     sibling = {"tm": me + 1 - 2 * core}
     across = {"tm": me + 2 - 4 * side}
-    later = {"tm": lax.rem(me + GROUP, count)}
-    earlier = {"tm": lax.rem(me + count - GROUP, count)}
-    return me, core, side, sibling, across, later, earlier, me + GROUP < count, me >= GROUP
+    later = [{"tm": lax.rem(me + n * GROUP, count)} for n in (1, 2)]
+    earlier = [{"tm": lax.rem(me + 2 * count - n * GROUP, count)} for n in (1, 2)]
+    has_later = [me + n * GROUP < count for n in (1, 2)]
+    has_earlier = [me >= n * GROUP for n in (1, 2)]
+    return me, core, side, sibling, across, later, earlier, has_later, has_earlier
 
 
 def kernel(
@@ -45,9 +48,9 @@
     projected, dq_out, dk_out, dv_out,
     q, k, v, grad, weights, mem, keys, values, bias, grad_t,
     query_t, key_own_t, own_probs, own_out, own_peak, own_grad, dq_part,
-    own, grads, landed, sums, totals, att, att_in, dq_buf, out_buf, projected_buf,
+    own, grads, landed_core, landed_side, landed_far, sums, totals, att, att_in,
     loads, gsend, greceive, bsend, breceive, wsend, wreceive, fsend, freceive,
-    asend, areceive, stores,
+    asend, areceive,
 ):
     me, core, side, sibling, across, later, earlier, has_later, has_earlier = place(count)
     head = lax.axis_index("head")
@@ -73,7 +76,7 @@
 
     peers = [{"head": lax.rem(head + n, parts)} for n in range(1, parts)]
     barrier = pltpu.get_barrier_semaphore()
-    neighbours = [sibling, across, later, earlier] + peers
+    neighbours = [sibling, across] + later + earlier + peers
     for device in neighbours:
         pl.semaphore_signal(barrier, inc=1, device_id=device, device_id_type=pl.DeviceIdType.MESH)
 
@@ -90,129 +93,140 @@
         for c in range(chunks):
             mem[c, 0, which] = mean[:, c * LANES : (c + 1) * LANES]
 
-    @pl.when(jnp.logical_not(has_earlier))
+    @pl.when(jnp.logical_not(has_earlier[0]))
     def _():
         for slot in (4, 8):
             for c in range(chunks):
                 mem[c, slot] = jnp.zeros(mem.shape[2:], BF16)
 
-    @pl.when(jnp.logical_not(has_later))
-    def _():
-        for number in (6, 7):
+    for n in range(2):
+        @pl.when(jnp.logical_not(has_later[n]))
+        def _():
             for c in range(chunks):
-                landed[c, number] = jnp.zeros(landed.shape[2:], BF16)
+                for which in range(2):
+                    landed_far[c, which, n] = jnp.zeros(landed_far.shape[3:], BF16)
 
     pl.semaphore_wait(barrier, len(neighbours))
 
-    def move(c, source, target, number, device):
+    arrivals = {4: 0, 8: 1, 2: 2, 6: 3, 1: 4, 3: 4, 5: 4, 7: 4}
+
+    def move(c, source, target, lane, arrival, device):
         return remote(
             mem.at[c, source], mem.at[c, target],
-            gsend.at[c, number], greceive.at[c, target], device,
+            gsend.at[c, lane], greceive.at[c, arrival], device,
         )
 
+    def to_later(c, source, target):
+        return move(c, source, target, 0, arrivals[target], later[0])
+
+    def to_across(c, source, target, arrival):
+        return move(c, source, target, 1, arrival, across)
+
+    def to_sibling(c, source, target):
+        return move(c, source, target, 2, 4, sibling)
+
     def arrive(c, slot):
-        move(c, slot, slot, 0, sibling).wait_recv()
+        move(c, slot, slot, 0, arrivals[slot], sibling).wait_recv()
 
     def send_own(c):
-        pl.when(has_later)(lambda: move(c, 0, 4, 0, later).start())
-        pl.when(side == 0)(lambda: move(c, 0, 2, 2, across).start())
-        pl.when(core == 0)(lambda: move(c, 0, 1, 4, sibling).start())
+        pl.when(has_later[0])(lambda: to_later(c, 0, 4).start())
+        pl.when(side == 0)(lambda: to_across(c, 0, 2, 2).start())
+        pl.when(core == 0)(lambda: to_sibling(c, 0, 1).start())
 
     def relay_four(c):
-        pl.when(has_earlier)(lambda: arrive(c, 4))
-        pl.when(has_later)(lambda: move(c, 4, 8, 1, later).start())
-        move(c, 4, 6 - 4 * side, 3 - side, across).start()
-        move(c, 4, 5 - 2 * core, 5 - core, sibling).start()
+        pl.when(has_earlier[0])(lambda: arrive(c, 4))
+        pl.when(has_later[0])(lambda: to_later(c, 4, 8).start())
+        to_across(c, 4, 6 - 4 * side, 3 - side).start()
+        to_sibling(c, 4, 5 - 2 * core).start()
 
     def relay_two_and_eight(c):
         arrive(c, 2)
-        move(c, 2, 3 - 2 * core, 6, sibling).start()
-        pl.when(has_earlier)(lambda: arrive(c, 8))
-        pl.when(side == 1)(lambda: move(c, 8, 6, 3, across).start())
-        pl.when(core == 1)(lambda: move(c, 8, 7, 5, sibling).start())
+        to_sibling(c, 2, 3 - 2 * core).start()
+        pl.when(has_earlier[0])(lambda: arrive(c, 8))
+        pl.when(side == 1)(lambda: to_across(c, 8, 6, 3).start())
+        pl.when(core == 1)(lambda: to_sibling(c, 8, 7).start())
 
     def relay_six(c):
         arrive(c, 6)
-        move(c, 6, 7 - 2 * core, 7, sibling).start()
+        to_sibling(c, 6, 7 - 2 * core).start()
+
+    def blocks_of(c, count_, lane, arrival):
+        some = mem.at[c, pl.ds(0, count_)]
+        return remote(some, some, gsend.at[c, lane], greceive.at[c, arrival], sibling)
 
     def gathered_all(c):
-        for slot in (1, 3, 5, 7):
-            arrive(c, slot)
+        blocks_of(c, 4, 2, 4).wait_recv()
 
     def gather_sent(c):
-        for number in (0, 1):
-            pl.when(has_later)(lambda: move(c, 0, 4, number, later).wait_send())
-        for number in range(2, 8):
-            move(c, 0, 2, number, across).wait_send()
-
-    def give(c, source, number, device):
-        return remote(
-            source, landed.at[c, number], bsend.at[c, number], breceive.at[c, number], device
-        )
-
-    def got(c, number):
-        give(c, grads.at[c, 0], number, sibling).wait_recv()
+        pl.when(has_later[0])(lambda: blocks_of(c, 2, 0, 0).wait_send())
+        blocks_of(c, 2, 1, 0).wait_send()
+        blocks_of(c, 4, 2, 0).wait_send()
+
+    def give(c, which, source, target, lane, device):
+        return remote(source, target, bsend.at[c, lane], breceive.at[c, which, lane], device)
+
+    def got(c, which, lane, target):
+        give(c, which, target, target, lane, sibling).wait_recv()
 
     is_core = core.astype(F32)
     is_side = side.astype(F32)
 
-    def term(c, number):
-        return landed[c, number].astype(F32)
-
-    def give_siblings(c):
-        for number, bottom, step in ((3, 5, 2), (1, 7, -2), (2, 1, 2), (0, 3, -2)):
-            give(c, grads.at[c, bottom + step * core - 1], number, sibling).start()
-
-    def give_across(c):
-        got(c, 3)
-        sums[c, 1] = (grads[c, 5].astype(F32) + term(c, 3)).astype(BF16)
-        give(c, sums.at[c, 1], 5, across).start()
-        got(c, 2)
-        sums[c, 0] = (grads[c, 1].astype(F32) + term(c, 2)).astype(BF16)
-        give(c, sums.at[c, 0], 4, across).start()
-
-    def give_eight(c):
-        got(c, 1)
-        got(c, 5)
-        total = grads[c, 7].astype(F32) + is_core * term(c, 1) + is_side * term(c, 5)
-        sums[c, 3] = total.astype(BF16)
-        pl.when(has_earlier)(lambda: give(c, sums.at[c, 3], 7, earlier).start())
-
-    def give_four(c):
-        got(c, 0)
-        got(c, 4)
-        total = grads[c, 3].astype(F32) + (1 - is_core) * term(c, 1) + is_core * term(c, 0)
-        total = total + (1 - is_side) * term(c, 5) + is_side * term(c, 4)
-        pl.when(has_later)(lambda: got(c, 7))
-        total = total + term(c, 7)
-        sums[c, 2] = total.astype(BF16)
-        pl.when(has_earlier)(lambda: give(c, sums.at[c, 2], 6, earlier).start())
+    def give_siblings(c, which):
+        give(c, which, grads.at[c, which, 0], landed_core.at[c, which], 0, sibling).start()
+
+    def give_across(c, which):
+        got(c, which, 0, landed_core.at[c, which])
+        for n, slot in ((0, 0), (1, 2)):
+            other = landed_core[c, which, 1 + slot - core].astype(F32)
+            sums[c, which, n] = (grads[c, which, 1, slot].astype(F32) + other).astype(BF16)
+        give(c, which, sums.at[c, which, pl.ds(0, 2)], landed_side.at[c, which], 1, across).start()
+
+    def give_earlier(c, which):
+        got(c, which, 1, landed_side.at[c, which])
+        far = landed_side[c, which, 1].astype(F32)
+        total = grads[c, which, 1, 3].astype(F32) + is_side * far
+        sums[c, which, 3] = (total + is_core * landed_core[c, which, 3].astype(F32)).astype(BF16)
+        pl.when(has_earlier[1])(
+            lambda: give(
+                c, which, sums.at[c, which, 3], landed_far.at[c, which, 1], 3, earlier[1]
+            ).start()
+        )
+        total = grads[c, which, 1, 1].astype(F32) + landed_core[c, which, 2 - core].astype(F32)
+        near = landed_side[c, which, 1 - side].astype(F32)
+        sums[c, which, 2] = (total + near).astype(BF16)
+        pl.when(has_earlier[0])(
+            lambda: give(
+                c, which, sums.at[c, which, 2], landed_far.at[c, which, 0], 2, earlier[0]
+            ).start()
+        )
 
     def columns(c):
         return pl.ds(pl.multiple_of(c * LANES, LANES), LANES)
 
-    def store(c, number, source, target):
-        return pltpu.make_async_copy(source, target.at[:, columns(c)], stores.at[c, number])
-
-    spread_token = lax.broadcasted_iota(jnp.int32, (tokens, pitch), 0)
-    spread_row = lax.broadcasted_iota(jnp.int32, (tokens, pitch), 1)
+    spread_token = lax.broadcasted_iota(jnp.int32, (pitch, tokens), 1)
+    spread_row = lax.broadcasted_iota(jnp.int32, (pitch, tokens), 0)
     spread_inside = (spread_token >= spread_row * POOL) & (spread_token < spread_row * POOL + POOL)
 
-    def finish(c):
-        pl.when(has_later)(lambda: got(c, 6))
-        total = (1 - is_core) * term(c, 0) + term(c, 6) + (1 - is_side) * term(c, 4)
+    def finish(c, which):
+        for n in range(2):
+            pl.when(has_later[n])(lambda: got(c, which, 2 + n, landed_far.at[c, which, n]))
+        total = (1 - is_core) * landed_core[c, which, 0].astype(F32)
+        total = total + (1 - is_side) * landed_side[c, which, 0].astype(F32)
+        for n in range(2):
+            total = total + landed_far[c, which, n].astype(F32)
         total = total.astype(BF16)
         spread = jnp.where(spread_inside, 1.0 / POOL, 0.0).astype(BF16)
-        for which, target in enumerate((dk_out, dv_out)):
-            shared = jnp.dot(spread, total[which], preferred_element_type=F32)
-            out_buf[c, which] = (own[c, which] + shared).astype(BF16)
-            store(c, which, out_buf.at[c, which], target).start()
+        shared = lax.dot_general(total, spread, BY_ROW, preferred_element_type=F32)
+        target = (dk_out, dv_out)[which]
+        target[:, columns(c)] = (own[c, which] + shared).astype(BF16).T
 
     def given(c):
-        for number in range(6):
-            give(c, grads.at[c, 0], number, sibling).wait_send()
-        for number in (6, 7):
-            pl.when(has_earlier)(lambda: give(c, grads.at[c, 0], number, sibling).wait_send())
+        give(c, 0, landed_core.at[c], landed_core.at[c], 0, sibling).wait_send()
+        give(c, 0, landed_side.at[c], landed_side.at[c], 1, sibling).wait_send()
+        for n in range(2):
+            pl.when(has_earlier[n])(
+                lambda: give(c, 0, landed_far.at[c, 0], landed_far.at[c, 0], 2 + n, sibling).wait_send()
+            )
 
     def weight_out(n):
         mine = weights.at[head, pl.ds(core * half, half)]
@@ -237,11 +251,15 @@
     def stacked(h, first, second):
         return jnp.concatenate([first, second] if h == 0 else [second, first], axis=0)
 
-    spare_line = lax.broadcasted_iota(jnp.int32, (HEAD_DIM, tokens), 0)
+    spare_line = lax.broadcasted_iota(jnp.int32, (16, tokens), 0)
+    blank = jnp.zeros((HEAD_DIM - 16, tokens), BF16)
+
+    def spared(first, second):
+        lines_ = jnp.where(spare_line == 0, first, jnp.where(spare_line == 1, second, 0.0))
+        return jnp.concatenate([lines_.astype(BF16), blank], axis=0)
 
     def query_side(c, h, level):
-        spare = jnp.where(spare_line == 0, level, 0.0).astype(BF16)
-        return stacked(h, query_t[c, lines(h), :], spare)
+        return stacked(h, query_t[c, lines(h), :], spared(level, 0.0))
 
     def weighted(h, value_t, low):
         moving = jnp.concatenate([value_t, jnp.ones((16, low.shape[0]), BF16)], axis=0)
@@ -251,8 +269,7 @@
         side = (grad_t[c, lines(h), :] * inverse).astype(BF16)
         high = delta.astype(BF16).astype(F32)
         low = delta - high
-        spare = jnp.where(spare_line == 0, -high, jnp.where(spare_line == 1, -low, 0.0)).astype(BF16)
-        return stacked(h, side, spare)
+        return stacked(h, side, spared(-high, -low))
 
     def marked(block, h, fill):
         lane = lax.broadcasted_iota(jnp.int32, block.shape, 1)
@@ -261,38 +278,51 @@
     def by_column(first, second):
         return lax.dot_general(first, second, BY_COLUMN, preferred_element_type=F32)
 
-    def own_forward(c, carry):
-        query_t[c] = (q[:, columns(c)] * scale).T
-        key = k[:, columns(c)]
-        key_own_t[c] = key.T
-        value_t = v[:, columns(c)].T
-        scores = [jnp.dot(key, query_side(c, h, 0.0), preferred_element_type=F32) for h in range(2)]
-        for h in range(2):
-            top = jnp.max(scores[h], axis=0, keepdims=True)
-            own_peak[c, h : h + 1, :] = top
-            low = jnp.exp(scores[h] - top).astype(BF16)
-            own_probs[c, h] = low
-            own_out[c, h] = weighted(h, value_t[lines(h), :], low)
-        return carry
-
-    def own_backward(c, carry):
-        value = v[:, columns(c)]
-        centred = []
-        for h in range(2):
-            centred.append(jnp.dot(marked(value, h, jnp.ones_like(value)), own_grad[c, h], preferred_element_type=F32))
-        dk, dv, dq = [], [], []
-        for h in range(2):
+    def own_forward(cs):
+        scores, value_t = {}, {}
+        for c in cs:
+            query_t[c] = (q[:, columns(c)] * scale).T
+            key = k[:, columns(c)]
+            key_own_t[c] = key.T
+            value_t[c] = v[:, columns(c)].T
+            for h in range(2):
+                scores[c, h] = jnp.dot(key, query_side(c, h, 0.0), preferred_element_type=F32)
+        for c in cs:
+            for h in range(2):
+                top = jnp.max(scores[c, h], axis=0, keepdims=True)
+                own_peak[c, h : h + 1, :] = top
+                low = jnp.exp(scores[c, h] - top).astype(BF16)
+                own_probs[c, h] = low
+                own_out[c, h] = weighted(h, value_t[c][lines(h), :], low)
+
+    def own_backward(cs):
+        heads = [(c, h) for c in cs for h in range(2)]
+        centred, grad_scores, dq = {}, {}, {}
+
+        def centre(c, h):
+            value = marked(v[:, columns(c)], h, jnp.ones((tokens, LANES), BF16))
+            centred[c, h] = jnp.dot(value, own_grad[c, h], preferred_element_type=F32)
+
+        def scored(c, h):
             low = own_probs[c, h]
-            grad_scores = (low.astype(F32) * centred[h]).astype(BF16)
-            dv.append(by_column(own_grad[c, h, lines(h), :], low))
-            dk.append(by_column(query_t[c, lines(h), :], grad_scores))
-            dq.append(jnp.dot(key_own_t[c, lines(h), :], grad_scores, preferred_element_type=F32))
-        for which, parts_ in enumerate((dk, dv)):
-            own[c, which] = jnp.concatenate(parts_, axis=0).T
-        total = jnp.concatenate(dq, axis=0) + dq_part[c]
-        dq_buf[c] = (total * scale).astype(BF16).T
-        store(c, 2, dq_buf.at[c], dq_out).start()
-        return carry
+            grad_scores[c, h] = (low.astype(F32) * centred[c, h]).astype(BF16)
+            own[c, 1, lines(h), :] = by_column(own_grad[c, h, lines(h), :], low)
+
+        def spent(c, h):
+            own[c, 0, lines(h), :] = by_column(query_t[c, lines(h), :], grad_scores[c, h])
+            dq[h] = jnp.dot(key_own_t[c, lines(h), :], grad_scores[c, h], preferred_element_type=F32)
+            if h == 1:
+                total = jnp.concatenate([dq[0], dq[1]], axis=0) + dq_part[c]
+                dq_out[:, columns(c)] = (total * scale).astype(BF16).T
+
+        centre(*heads[0])
+        for n, pair in enumerate(heads):
+            if n + 1 < len(heads):
+                centre(*heads[n + 1])
+            scored(*pair)
+            if n > 0:
+                spent(*heads[n - 1])
+        spent(*heads[-1])
 
     for c in range(min(2, chunks)):
         send_own(c)
@@ -305,11 +335,11 @@
     ).reshape(grad_t.shape)
     inputs[4].wait()
     middle = chunks // 2
-    lax.fori_loop(0, middle, own_forward, 0)
+    own_forward(range(middle, chunks))
     relay_four(0)
     if chunks > 2:
         send_own(2)
-    lax.fori_loop(middle, chunks, own_forward, 0)
+    own_forward(range(middle))
     if chunks > 1:
         relay_four(1)
     for c in range(3, chunks):
@@ -394,11 +424,10 @@
             part = jnp.dot(key_t[lines(h), blocks[n]], gs[h, n], preferred_element_type=F32)
             dq[h] = part if n == 0 else dq[h] + part
 
-        def give_block(n):
-            for which in range(2):
-                both = totals[which, :, blocks[n]].astype(BF16).T
-                for slot in range(2):
-                    grads[i, 2 * n + slot, which] = both[slot * pitch : (slot + 1) * pitch, :]
+        def give_block(n, which):
+            both = totals[which, :, blocks[n]].astype(BF16).T
+            for slot in range(2):
+                grads[i, which, slot, n] = both[slot * pitch : (slot + 1) * pitch, :]
 
         for n in range(count_):
             score(0, n)
@@ -422,15 +451,13 @@
 
         @pl.when(i > 0)
         def _():
-            give_across(i - 1)
+            for which in (1, 0):
+                give_across(i - 1, which)
 
         @pl.when(i > 1)
         def _():
-            give_eight(i - 2)
-
-        @pl.when(i > 2)
-        def _():
-            give_four(i - 3)
+            for which in (1, 0):
+                give_earlier(i - 2, which)
 
         centre(0, 0)
         for n in range(count_):
@@ -450,21 +477,25 @@
         for n in range(1, parts):
             attended_out(i, n).start()
 
+        for n in range(count_):
+            value_grad(1, n)
         centre(1, 0)
+        for n in range(count_):
+            give_block(n, 1)
+        give_siblings(i, 1)
         for n in range(count_):
             if n + 1 < count_:
                 centre(1, n + 1)
-            value_grad(1, n)
             grad_score(1, n)
             if n > 0:
                 key_grad(1, n - 1)
+                give_block(n - 1, 0)
         key_grad(1, count_ - 1)
-        for n in range(count_):
-            give_block(n)
-        give_siblings(i)
+        give_block(count_ - 1, 0)
+        give_siblings(i, 0)
         dq_part[i] = jnp.concatenate([dq[0], dq[1]], axis=0)
 
-        @pl.when(i == min(1, chunks - 1))
+        @pl.when(i == min(2, chunks - 1))
         def _():
             for n in range(1, parts):
                 weight_out(n).wait_recv()
@@ -476,19 +507,17 @@
     lax.fori_loop(0, chunks, step, 0)
 
     last = chunks - 1
+    own_backward(range(middle, chunks))
+    for which in (1, 0):
+        give_across(last, which)
     if chunks > 1:
-        give_eight(last - 1)
-    if chunks > 2:
-        give_four(last - 2)
-    lax.fori_loop(0, middle, own_backward, 0)
-    give_across(last)
-    if chunks > 1:
-        give_four(last - 1)
-    lax.fori_loop(middle, chunks, own_backward, 0)
-    for c in range(chunks - 2):
-        finish(c)
-    give_eight(last)
+        for which in (1, 0):
+            give_earlier(last - 1, which)
+    if middle > 0:
+        own_backward(range(middle))
     total = jnp.dot(att[head], weights[head], preferred_element_type=F32)
+    for which in (1, 0):
+        give_earlier(last, which)
     for n in range(1, parts):
         weight_on(n).wait_recv()
         for c in range(chunks):
@@ -496,26 +525,19 @@
     for n in range(1, parts):
         other = lax.rem(head + n, parts)
         total = total + jnp.dot(att_in[other], weights[other], preferred_element_type=F32)
-    projected_buf[...] = total.astype(BF16)
-    final = pltpu.make_async_copy(projected_buf, projected, loads.at[5])
-    final.start()
-    if chunks > 1:
-        finish(last - 1)
-    give_four(last)
-    for c in range(chunks - 1):
+    projected[...] = total.astype(BF16)
+    for c in range(last):
+        for which in (1, 0):
+            finish(c, which)
         given(c)
-        for number in range(3):
-            store(c, number, dq_buf.at[c], dq_out).wait()
     for n in range(1, parts):
         weight_out(n).wait_send()
         weight_on(n).wait_send()
         for c in range(chunks):
             attended_out(c, n).wait_send()
-    finish(last)
+    for which in (1, 0):
+        finish(last, which)
     given(last)
-    for number in range(3):
-        store(last, number, dq_buf.at[last], dq_out).wait()
-    final.wait()
 
 
 def whole(queries, key_tokens, value_tokens, out_weight, out_grad, start, count, parts):
@@ -554,39 +576,59 @@
             pltpu.VMEM((chunks, 2, tokens), F32),
             pltpu.VMEM((chunks, 2, LANES, tokens), BF16),
             pltpu.VMEM((chunks, LANES, tokens), F32),
-            pltpu.VMEM((chunks, 2, tokens, LANES), F32),
-            pltpu.VMEM((chunks, MEM, 2, pitch, LANES), BF16),
-            pltpu.VMEM((chunks, 8, 2, pitch, LANES), BF16),
-            pltpu.VMEM((chunks, 4, 2, pitch, LANES), BF16),
+            pltpu.VMEM((chunks, 2, LANES, tokens), F32),
+            pltpu.VMEM((chunks, 2, 2, MEM // 2, pitch, LANES), BF16),
+            pltpu.VMEM((chunks, 2, MEM // 2, pitch, LANES), BF16),
+            pltpu.VMEM((chunks, 2, 2, pitch, LANES), BF16),
+            pltpu.VMEM((chunks, 2, 2, pitch, LANES), BF16),
+            pltpu.VMEM((chunks, 2, 4, pitch, LANES), BF16),
             pltpu.VMEM((2, LANES, MEM * pitch), F32),
             pltpu.VMEM((parts, rows, width), BF16),
             pltpu.VMEM((parts, rows, width), BF16),
-            pltpu.VMEM((chunks, tokens, LANES), BF16),
-            pltpu.VMEM((chunks, 2, tokens, LANES), BF16),
-            pltpu.VMEM((rows, full), BF16),
-            dma((6,)),
-            dma((chunks, 8)),
-            dma((chunks, MEM + 1)),
-            dma((chunks, 8)),
-            dma((chunks, 8)),
+            dma((5,)),
+            dma((chunks, 3)),
+            dma((chunks, 5)),
+            dma((chunks, 4)),
+            dma((chunks, 2, 4)),
             dma((parts - 1,)),
             dma((parts - 1,)),
             dma((parts - 1,)),
             dma((parts - 1,)),
             dma((chunks, parts - 1)),
             dma((chunks, parts - 1)),
-            dma((chunks, 3)),
         ],
         compiler_params=pltpu.CompilerParams(collective_id=1, has_side_effects=True),
         name="attention",
     )(start, queries, key_tokens, value_tokens, out_weight, out_grad)
 
 
+def copy_kernel(*refs):
+    count = len(refs) // 2
+    done = refs[-1]
+    copies = [pltpu.make_async_copy(refs[n], refs[count + n], done.at[n]) for n in range(count)]
+    for copy in copies:
+        copy.start()
+    for copy in copies:
+        copy.wait()
+
+
+def copied(arrays):
+    return pl.pallas_call(
+        copy_kernel,
+        in_specs=[pl.BlockSpec(memory_space=pltpu.VMEM)] * len(arrays),
+        out_specs=[pl.BlockSpec(memory_space=pl.ANY)] * len(arrays),
+        out_shape=[jax.ShapeDtypeStruct(array.shape, array.dtype) for array in arrays],
+        scratch_shapes=[pltpu.SemaphoreType.DMA((len(arrays),))],
+        name="copied",
+    )(*[pltpu.with_memory_space_constraint(array, pltpu.VMEM) for array in arrays])
+
+
 def local(queries, key_tokens, value_tokens, out_weight, out_grad, clip_starts):
-    projected, dq, dk, dv = whole(
+    outputs = whole(
         queries[0], key_tokens[0], value_tokens[0], out_weight, out_grad[0], clip_starts,
         lax.axis_size("tm"), lax.axis_size("head"),
     )
+    projected, dq, dk, dv = copied(outputs)
     return (projected[None], dq[None], dk[None], dv[None])
 
 

time: 51 us -> 47.5 us (0.931)
  local copies, waits for them, and re-layouts: 3 us -> 0 us
    unnamed x4 -> x0, local copies, waits for them, and re-layouts: 3 us -> none
    pallas_call x1, Pallas kernels: 46.5 us -> 44.9 us  [whole(): pl.pallas_call(functools.partial(kernel, count, parts), in_specs=[pl.Bloc...]
    pallas_call x0 -> x1, Pallas kernels: none -> 1.19 us  [copied(): pl.pallas_call(copy_kernel, in_specs=[pl.BlockSpec(memory_space=pltpu.VME...]
where the time goes in v4:
time: 47.5 us; the launch traced here: 47.4 us
  Pallas kernels  46.1 us (97%)
  between operations  1.29 us (3%)
    pallas_call x1, Pallas kernels, whole(): pl.pallas_call(functools.partial(kernel, count, parts), in_specs=[pl.Bloc...  44.9 us
    pallas_call x1, Pallas kernels, copied(): pl.pallas_call(copy_kernel, in_specs=[pl.BlockSpec(memory_space=pltpu.VME...  1.19 us

profile of v4, /device:TPU:0, one launch (start us, length us, event | category | flops | bytes accessed | tf_op | source)
XLA Modules:
  0.0 47.4 jit_solution(10627731142260529529)
XLA Ops:
  1.3 44.9 %attention.1 = (bf16[196,1024]{1,0:T(8,128)(2,1)S(1)}, bf16[392,512]{1,0:T(8,128)(2,1)S(1)}, bf16[392,512]{1,0:T(8,128)(2,1)S(1)}, bf16[392,512]{1,0:T(8,128)(2,1)S(1)}) custom-call(s32[1]{0:T(128)S(6)} %copy.10.start, bf16[392,512]{1,0:T(8,128)(2,1)} %bitcast.9, bf16[392,512]{1,0:T(8,128)(2,1)} %bitcast.10, bf16[392,512]{1,0:T(8,128)(2,1)} %bitcast.11, ...), custom_call_target="tpu_custom_call" | custom-call | tf_op jit(solution)/shard_map/attention/pallas_call | solution.py:551
  46.2 1.2 %copied.1 = (bf16[196,1024]{1,0:T(8,128)(2,1)}, bf16[392,512]{1,0:T(8,128)(2,1)}, bf16[392,512]{1,0:T(8,128)(2,1)}, bf16[392,512]{1,0:T(8,128)(2,1)}) custom-call(bf16[196,1024]{1,0:T(8,128)(2,1)S(1)} %get-tuple-element.12.refs_0_, bf16[392,512]{1,0:T(8,128)(2,1)S(1)} %get-tuple-element.13.refs_1_, bf16[392,512]{1,0:T(8,128)(2,1)S(1)} %get-tuple-element.14.refs_2_, ...), custom_call_target="tpu_custom_call" | custom-call | tf_op jit(solution)/shard_map/copied/pallas_call | solution.py:616
